TPU v7x, 256 devices: a whole 4x4x8 slice. The times are simulated.
256 devices in a mesh: tm: 16 (over z_lo, x), chan: 16 (over z_hi, y, core).
Axes of the slice: x: 4, y: 4, z: 8 (z_hi: 2, z_lo: 4; z = z_hi * 4 + z_lo), core: 2. Of those that a mesh axis runs over, the one named last changes fastest.
Arguments:
- traces: float32 [4096, 16384], P('tm', 'chan'), may hold values from -6 to 6
- band_edges: int32 [2, 4096], replicated, may hold values from 0 to 8191, as said below
- taps: float32 [255], replicated, may hold values from -0.375 to 0.375
- gain_table: float32 [64], replicated, may hold values from 0.3 to 3
- gain_index: int32 [16384], P('chan'), may hold values from 0 to 63
Outputs:
- filtered: float32 [4096, 16384], P('tm', 'chan')
Inputs may be any that keep to these rules, and one draw needn't show every extreme that they name: band_edges[0, f] <= band_edges[1, f] for every f.
All inputs are finite; a program needn't handle non-finite values.
Results may differ from a plain program's by a relative error of at most 0.0001.
Values sent between devices are 32-bit elements; how exact they have to be, the bound alone decides.
No kernel may reach another device: no remote copies, remote signals or barrier semaphores. Data moves between devices by JAX's collectives and lax.ppermute only.
A program may use at most 128 MiB of HBM per device.

v0:
```python
import math

import jax
import jax.numpy as jnp
import numpy as np
from jax import lax
from jax.experimental import pallas as pl
from jax.experimental.pallas import tpu as pltpu
from jax.sharding import PartitionSpec as P

f32 = jnp.float32
bf16 = jnp.bfloat16


def circle(product, period):
    theta = (product % period).astype(np.float64) * (2.0 * math.pi / period)
    return np.cos(theta), np.sin(theta)


def halves(table):
    table = np.asarray(table, np.float64)
    high = table.astype(np.float32).astype(jnp.bfloat16)
    low = (table - high.astype(np.float64)).astype(np.float32).astype(jnp.bfloat16)
    return high, low


def channel_tables():
    n = np.arange(128)
    cos, sin = circle(n[:, None] * n[None, :], 128)
    turn_cos, turn_sin = circle(n[:, None] * n[None, :], 16384)
    first = np.concatenate([cos, -sin], axis=0)
    second = np.zeros((2, 128, 2, 2, 32))
    for h in range(2):
        c, s = cos[:, 32 * h : 32 * h + 32], sin[:, 32 * h : 32 * h + 32]
        second[0, :, h, 0], second[1, :, h, 0] = c, s
        second[0, :, h, 1], second[1, :, h, 1] = -s, c
    second = second.reshape(256, 128)
    return first, second, turn_cos.astype(np.float32), turn_sin.astype(np.float32)


def time_tables():
    n = np.arange(128)
    cos, sin = circle(n[:, None] * n[None, :], 128)
    forward = np.block([[cos, sin], [-sin, cos]])
    f1 = np.arange(1024) // 32
    turn_cos, turn_sin = circle(n[:, None] * f1[None, :], 4096)
    f0 = (np.arange(128) // 32) % 2
    m = np.arange(16)
    early_cos, early_sin = circle(m[:, None] * f0[None, :], 32)
    shift_cos, shift_sin = circle(f1[None, :], 32)
    single = lambda *arrays: [np.asarray(a, np.float32) for a in arrays]
    return forward, single(turn_cos, turn_sin, early_cos, early_sin, shift_cos, shift_sin)


def split(x):
    high = x.astype(bf16)
    return high, (x - high.astype(f32)).astype(bf16)


def mm(a, b):
    return jnp.dot(a, b, preferred_element_type=f32)


def left(table_high, table_low, x):
    high, low = split(x)
    return mm(table_high, high) + (mm(table_high, low) + mm(table_low, high))


def right(x, table_high, table_low):
    high, low = split(x)
    return mm(high, table_high) + (mm(low, table_high) + mm(high, table_low))


def lane_bit(rows, bit):
    lane = lax.broadcasted_iota(jnp.int32, (rows, 128), 1)
    return (lane & bit) != 0


def exchange(a, b, mask, bit):
    rolled_b = pltpu.roll(b, bit, 1)
    rolled_a = pltpu.roll(a, 128 - bit, 1)
    return jnp.where(mask, rolled_b, a), jnp.where(mask, b, rolled_a)


def rotate(re, im, angle_num, angle_den, sign):
    num = (angle_num * 8) / angle_den
    if num == 0:
        return re, im
    if num == 2:
        return (im, -re) if sign < 0 else (-im, re)
    if num == 1 or num == 3:
        root = math.sqrt(0.5)
        if sign < 0:
            a, b = (re + im, im - re) if num == 1 else (im - re, -re - im)
        else:
            a, b = (re - im, im + re) if num == 1 else (-re - im, re - im)
        return a * root, b * root
    c = math.cos(2 * math.pi * angle_num / angle_den)
    s = sign * math.sin(2 * math.pi * angle_num / angle_den)
    return re * c - im * s, im * c + re * s


def small_fft(re, im, sign):
    n = len(re)
    if n == 1:
        return re, im
    er, ei = small_fft(re[0::2], im[0::2], sign)
    odd_r, odd_i = small_fft(re[1::2], im[1::2], sign)
    out_r, out_i = [None] * n, [None] * n
    for k in range(n // 2):
        tr, ti = rotate(odd_r[k], odd_i[k], k, n, sign)
        out_r[k], out_i[k] = er[k] + tr, ei[k] + ti
        out_r[k + n // 2], out_i[k + n // 2] = er[k] - tr, ei[k] - ti
    return out_r, out_i


def channel_forward(x, first_h, first_l, second_h, second_l, cos, sin, out):
    mask = lane_bit(128, 64)
    for rl in range(8):
        blocks = []
        for rh in range(2):
            rows = [x[pl.ds(j * 128 + rh * 64 + rl, 8, stride=8), :] for j in range(16)]
            blocks.append(jnp.concatenate(rows, axis=0))
        y = left(first_h[...], first_l[...], jnp.concatenate(blocks, axis=1))
        turned = []
        for rh in range(2):
            yr = y[:128, 128 * rh : 128 * rh + 128]
            yi = y[128:, 128 * rh : 128 * rh + 128]
            c, s = cos[...], sin[...]
            turned.append(jnp.concatenate([yr * c + yi * s, yi * c - yr * s], axis=1))
        o = right(jnp.concatenate(turned, axis=0), second_h[...], second_l[...])
        low, high = exchange(o[:128], o[128:], mask, 64)
        out[pl.ds(rl, 128, stride=16), :] = low
        out[pl.ds(8 + rl, 128, stride=16), :] = high


def channel_inverse(x, first_h, first_l, second_h, second_l, cos, sin, out):
    mask = lane_bit(128, 64)
    for rl in range(8):
        low = x[pl.ds(rl, 128, stride=16), :]
        high = x[pl.ds(8 + rl, 128, stride=16), :]
        pair = exchange(low, high, mask, 64)
        u = right(jnp.concatenate(pair, axis=0), second_h[...], second_l[...])
        turned = []
        for rh in range(2):
            ur = u[128 * rh : 128 * rh + 128, :128]
            ui = u[128 * rh : 128 * rh + 128, 128:]
            c, s = cos[...], sin[...]
            turned.append(jnp.concatenate([ur * c - ui * s, ui * c + ur * s], axis=0))
        o = left(first_h[...], first_l[...], jnp.concatenate(turned, axis=1))
        for rh in range(2):
            for j in range(16):
                out[pl.ds(j * 128 + rh * 64 + rl, 8, stride=8), :] = o[
                    8 * j : 8 * j + 8, 128 * rh : 128 * rh + 128
                ]


def time_part(
    x, factor, fir, fwd_h, fwd_l, inv_h, inv_l, cos2, sin2, cos1, sin1, cos3, sin3,
    out, work, past, future,
):
    bit32, bit64 = lane_bit(8, 32), lane_bit(8, 64)
    for jl in range(8):
        tiles = [x[th * 64 + jl * 8 : th * 64 + jl * 8 + 8, :] for th in range(32)]
        re, im = [], []
        for m in range(16):
            r, i = exchange(tiles[m] + tiles[m + 16], tiles[m] - tiles[m + 16], bit32, 32)
            if m > 0:
                c, s = cos1[m : m + 1, :], sin1[m : m + 1, :]
                r, i = r * c + i * s, i * c - r * s
            re.append(r)
            im.append(i)
        re, im = small_fft(re, im, -1)
        for part, values in ((0, re), (1, im)):
            for g in range(8):
                for rh, value in enumerate(exchange(values[2 * g], values[2 * g + 1], bit64, 64)):
                    row = part * 128 + jl * 16 + rh * 8
                    work[row : row + 8, g * 128 : g * 128 + 128] = value

    fir_h, fir_l = split(fir[...])
    for step in range(4):
        cols = slice(256 * step, 256 * step + 256)
        c, s = cos2[:, cols], sin2[:, cols]
        re, im = work[:128, cols], work[128:, cols]
        b = jnp.concatenate([re * c + im * s, im * c - re * s], axis=0)
        spectrum = left(fwd_h[...], fwd_l[...], b)
        kept = factor[:, cols]
        spectrum = jnp.concatenate([spectrum[:128] * kept, spectrum[128:] * kept], axis=0)
        z = left(inv_h[...], inv_l[...], spectrum)
        re, im = z[:128], z[128:]
        z = jnp.concatenate([re * c - im * s, im * c + re * s], axis=1)
        v = left(fir_h, fir_l, z)
        same, before, after = v[:128], v[128:256], v[256:]
        total, differ = before + after, after - before
        c, s = cos3[:, cols], sin3[:, cols]
        work[:128, cols] = same[:, :256] + (total[:, :256] * c - differ[:, 256:] * s)
        work[128:, cols] = same[:, 256:] + (total[:, 256:] * c + differ[:, :256] * s)
        br, bi = before[:, :256], before[:, 256:]
        wr, wi = br * c + bi * s, bi * c - br * s
        wrapped = jnp.concatenate([wr[:, :128] + wr[:, 128:], wi[:, :128] + wi[:, 128:]], axis=1)
        ahead = jnp.concatenate(
            [after[:, :128] + after[:, 128:256], after[:, 256:384] + after[:, 384:]], axis=1
        )
        if step == 0:
            past[...] = wrapped
            future[...] = ahead
        else:
            past[...] += wrapped
            future[...] += ahead

    for jl in range(8):
        parts = []
        for part in range(2):
            values = [None] * 16
            row = part * 128 + jl * 16
            for g in range(8):
                cols = slice(g * 128, g * 128 + 128)
                values[2 * g], values[2 * g + 1] = exchange(
                    work[row : row + 8, cols], work[row + 8 : row + 16, cols], bit64, 64
                )
            parts.append(values)
        re, im = small_fft(parts[0], parts[1], 1)
        edges = []
        for ref in (past, future):
            sums = []
            for rh in range(2):
                for part in range(2):
                    row = jl * 16 + rh * 8
                    e = ref[row : row + 8, part * 128 : part * 128 + 128]
                    e = e + pltpu.roll(e, 64, 1)
                    sums.append(e + pltpu.roll(e, 32, 1))
            edges.append(
                jnp.where(
                    bit64,
                    jnp.where(bit32, sums[3], sums[2]),
                    jnp.where(bit32, sums[1], sums[0]),
                )
            )
        for m in range(16):
            r, i = re[m], im[m]
            if m > 0:
                c, s = cos1[m : m + 1, :], sin1[m : m + 1, :]
                r, i = r * c - i * s, i * c + r * s
            even, odd = exchange(r, i, bit32, 32)
            early, late = even + odd, even - odd
            if m == 0:
                early = early - edges[0]
            if m == 15:
                late = late - edges[1]
            out[m * 64 + jl * 8 : m * 64 + jl * 8 + 8, :] = early
            out[(m + 16) * 64 + jl * 8 : (m + 16) * 64 + jl * 8 + 8, :] = late


def call(body, args, scratch=()):
    return pl.pallas_call(
        body,
        out_shape=jax.ShapeDtypeStruct((2048, 128), f32),
        in_specs=[pl.BlockSpec(memory_space=pltpu.VMEM)] * len(args),
        out_specs=pl.BlockSpec(memory_space=pltpu.VMEM),
        scratch_shapes=list(scratch),
        compiler_params=pltpu.CompilerParams(vmem_limit_bytes=40 * 1024 * 1024),
        name=body.__name__,
    )(*args)


def forward_kernel(x):
    first, second, cos, sin = channel_tables()
    return call(channel_forward, (x, *halves(first), *halves(second), cos, sin))


def inverse_kernel(x):
    first, second, cos, sin = channel_tables()
    return call(channel_inverse, (x, *halves(first.T), *halves(second.T), cos, sin))


def time_kernel(x, factor, fir):
    forward, tables = time_tables()
    args = (x, factor, fir, *halves(forward), *halves(forward.T), *tables)
    scratch = (
        pltpu.VMEM((256, 1024), f32),
        pltpu.VMEM((128, 256), f32),
        pltpu.VMEM((128, 256), f32),
    )
    return call(time_part, args, scratch)


def fir_matrix(taps):
    padded = jnp.concatenate([jnp.zeros((1,), f32), taps, jnp.zeros((129,), f32)])
    wide = jnp.tile(padded, 128)[: 128 * 384].reshape(128, 384)
    return jnp.concatenate([wide[:, 128:256], wide[:, :128], wide[:, 256:]], axis=0)


def mask_factor(band_edges, owner, scale):
    spread = np.repeat(np.eye(32, dtype=np.float32), 32, axis=1)
    edges = band_edges.astype(f32).reshape(256, 32)
    edges = jnp.dot(edges, spread, precision=lax.Precision.HIGHEST)
    kl = jnp.arange(1024, dtype=jnp.int32) % 32
    wave = owner // 2 + 128 * (32 * (owner % 2) + kl)
    wave_f = wave.astype(f32)[None, :]
    kept = (wave_f >= edges[:128]) & (wave_f <= edges[128:])
    weight = jnp.where(wave == 0, scale, 2.0 * scale).astype(f32)[None, :]
    return jnp.where(kept, weight, 0.0)


def per_device(traces, band_edges, taps, gain_table, gain_index):
    both = ("tm", "chan")
    owner = lax.axis_index("tm") * 16 + lax.axis_index("chan")
    factor = mask_factor(band_edges, owner, 1.0 / (4096 * 16384))
    fir = fir_matrix(taps)
    matches = gain_index[:, None] == jnp.arange(64, dtype=jnp.int32)[None, :]
    gains = jnp.sum(jnp.where(matches, gain_table[None, :], 0.0), axis=1)

    x = traces.reshape(16, 2, 8, 8, 128).transpose(0, 1, 3, 2, 4).reshape(16, 128, 128)
    x = lax.all_to_all(x, "chan", 0, 0, tiled=True).reshape(2048, 128)
    x = forward_kernel(x).reshape(256, 8, 128)
    x = lax.all_to_all(x, both, 0, 0, tiled=True).reshape(2048, 128)
    x = time_kernel(x, factor, fir).reshape(256, 8, 128)
    x = lax.all_to_all(x, both, 0, 0, tiled=True).reshape(2048, 128)
    x = inverse_kernel(x).reshape(16, 128, 128)
    x = lax.all_to_all(x, "chan", 0, 0, tiled=True)
    x = x.reshape(16, 2, 8, 8, 128).transpose(0, 1, 3, 2, 4).reshape(256, 1024)
    return x * gains[None, :]


def solution(mesh):
    in_specs = (P("tm", "chan"), P(), P(), P(), P("chan"))
    return jax.shard_map(
        per_device, mesh=mesh, in_specs=in_specs, out_specs=P("tm", "chan"), check_vma=False
    )
```

profile of v0, /device:TPU:33, one launch (start us, length us, event | category | flops | bytes accessed | tf_op | source)
XLA Modules:
  0.0 168.2 jit_solution(10964395370445413413)
XLA Ops:
  0.0 0.0 copy-start.13
  0.0 0.0 copy-start.14
  0.0 0.0 copy-start.15
  0.0 41.6 %all_to_all.20 = f32[16,128,128]{2,1,0:T(8,128)S(1)} all-to-all(f32[16,128,128]{2,1,0:T(8,128)} %bitcast.25), channel_id=1, replica_groups=mesh['tm'=16,'chan'=16] {'chan'}, dimensions={0} | all-to-all | bytes 2097152 | tf_op jit(solution)/shard_map/all_to_all | solution.py:314
  41.6 0.0 copy-done.2
  41.6 0.0 copy-done.3
  41.6 0.0 copy-done.12
  41.6 0.0 copy-done.13
  41.6 0.0 copy-done.14
  41.7 0.0 copy-done.15
  41.7 3.4 %channel_forward.1 = f32[2048,128]{1,0:T(8,128)} custom-call(f32[2048,128]{1,0:T(8,128)S(1)} %bitcast.21, bf16[256,128]{1,0:T(8,128)(2,1)S(1)} %copy-done.12, bf16[256,128]{1,0:T(8,128)(2,1)S(1)} %copy-done.13, bf16[256,128]{1,0:T(8,128)(2,1)S(1)} %copy-done.14, bf16[256,128]{1,0:T(8,128)(2,1)S(1)} %copy-done.15, f32[128,128]{1,0:T(8,128)S(1)} %copy-done.2, ...), custom_call_target="tpu_custom_call" | custom-call | tf_op jit(solution)/shard_map/channel_forward/pallas_call | solution.py:255
  45.1 8.2 %all-to-all-start.1 = ((f32[256,8,128]{2,1,0:T(8,128)}), f32[256,8,128]{2,1,0:T(8,128)S(1)}, u32[]{:S(2)}, u32[]{:S(2)}) async-start(f32[256,8,128]{2,1,0:T(8,128)} %bitcast.4), calls=%async_computation.1 | async-start | bytes 2097152 | tf_op jit(solution)/shard_map/all_to_all | solution.py:316
  53.3 0.0 copy-start.21
  53.3 0.7 copy-done.21
  54.0 0.1 reshape.62
  54.2 0.0 copy-start.23
  54.2 0.7 copy-done.23
  54.9 0.1 pad_maximum_fusion.1
  55.0 0.3 tile.10
  55.5 0.0 copy-start.20
  55.5 0.9 copy-done.20
  56.4 1.0 convolution_bitcast_fusion
  57.3 0.0 copy-start
  57.4 0.0 copy-start.1
  57.4 0.0 copy-start.4
  57.4 0.0 copy-start.5
  57.4 0.0 copy-start.6
  57.4 0.0 copy-start.7
  57.4 0.0 copy-start.16
  57.4 0.1 fusion.1.factor
  57.5 26.0 %all-to-all-done.1 = f32[256,8,128]{2,1,0:T(8,128)S(1)} async-done(((f32[256,8,128]{2,1,0:T(8,128)}), f32[256,8,128]{2,1,0:T(8,128)S(1)}, u32[]{:S(2)}, u32[]{:S(2)}) %all-to-all-start.1) | async-done | bytes 1048608 | tf_op jit(solution)/shard_map/all_to_all | solution.py:316
  83.5 0.0 copy-done.17
  83.5 0.0 copy-done.18
  83.5 0.0 copy-done.19
  83.5 0.0 copy-done
  83.5 0.0 copy-done.1
  83.6 5.3 %time_part.1 = f32[2048,128]{1,0:T(8,128)S(1)} custom-call(f32[2048,128]{1,0:T(8,128)S(1)} %bitcast.22, f32[128,1024]{1,0:T(8,128)S(1)} %fusion.1.factor, f32[384,128]{1,0:T(8,128)S(1)} %pad_maximum_fusion.fir, bf16[256,256]{1,0:T(8,128)(2,1)S(1)} %copy-done.4, bf16[256,256]{1,0:T(8,128)(2,1)S(1)} %copy-done.5, bf16[256,256]{1,0:T(8,128)(2,1)S(1)} %copy-done.6, ...), custom_call_target="tpu_custom_call" | custom-call | tf_op jit(solution)/shard_map/time_part/pallas_call | solution.py:255
  88.8 0.0 copy-start.8
  88.8 0.0 copy-start.9
  88.8 0.0 copy-start.10
  88.9 0.0 copy-start.11
  88.9 37.1 %all_to_all.21 = f32[256,8,128]{2,1,0:T(8,128)S(1)} all-to-all(f32[256,8,128]{2,1,0:T(8,128)S(1)} %bitcast.23), channel_id=1, replica_groups=mesh['tm'=16,'chan'=16] {'tm','chan'}, dimensions={0} | all-to-all | bytes 2097152 | tf_op jit(solution)/shard_map/all_to_all | solution.py:318
  126.0 0.0 copy-done.11
  126.0 4.7 %channel_inverse.1 = f32[2048,128]{1,0:T(8,128)} custom-call(f32[2048,128]{1,0:T(8,128)S(1)} %bitcast.20, bf16[128,256]{1,0:T(8,128)(2,1)S(1)} %copy-done.8, bf16[128,256]{1,0:T(8,128)(2,1)S(1)} %copy-done.9, bf16[128,256]{1,0:T(8,128)(2,1)S(1)} %copy-done.10, bf16[128,256]{1,0:T(8,128)(2,1)S(1)} %copy-done.11, f32[128,128]{1,0:T(8,128)S(1)} %copy-done.2, ...), custom_call_target="tpu_custom_call" | custom-call | tf_op jit(solution)/shard_map/channel_inverse/pallas_call | solution.py:255
  130.7 5.5 %all-to-all-start.3 = ((f32[16,128,128]{2,1,0:T(8,128)}), f32[16,128,128]{2,1,0:T(8,128)S(1)}, u32[]{:S(2)}, u32[]{:S(2)}) async-start(f32[16,128,128]{2,1,0:T(8,128)} %bitcast.9), calls=%async_computation.3 | async-start | bytes 2097152 | tf_op jit(solution)/shard_map/all_to_all | solution.py:320
  136.3 0.1 select_reduce_fusion
  136.4 30.7 %all-to-all-done.3 = f32[16,128,128]{2,1,0:T(8,128)S(1)} async-done(((f32[16,128,128]{2,1,0:T(8,128)}), f32[16,128,128]{2,1,0:T(8,128)S(1)}, u32[]{:S(2)}, u32[]{:S(2)}) %all-to-all-start.3) | async-done | bytes 1048608 | tf_op jit(solution)/shard_map/all_to_all | solution.py:320
  167.1 1.1 broadcast_multiply_fusion
  (27 shorter events, 0.2 us)
Async XLA Ops:
  0.0 41.6 %copy-start.2 = (f32[128,128]{1,0:T(8,128)S(1)}, f32[128,128]{1,0:T(8,128)}, u32[]{:S(2)}) copy-start(f32[128,128]{1,0:T(8,128)} %constant.107.clone.cos) | copy-start | bytes 196612
  0.0 41.6 %copy-start.3 = (f32[128,128]{1,0:T(8,128)S(1)}, f32[128,128]{1,0:T(8,128)}, u32[]{:S(2)}) copy-start(f32[128,128]{1,0:T(8,128)} %constant.108.clone.sin) | copy-start | bytes 196612
  0.0 41.6 %copy-start.12 = (bf16[256,128]{1,0:T(8,128)(2,1)S(1)}, bf16[256,128]{1,0:T(8,128)(2,1)}, u32[]{:S(2)}) copy-start(bf16[256,128]{1,0:T(8,128)(2,1)} %constant.103.clone.first_h) | copy-start | bytes 196612
  0.0 41.6 %copy-start.13 = (bf16[256,128]{1,0:T(8,128)(2,1)S(1)}, bf16[256,128]{1,0:T(8,128)(2,1)}, u32[]{:S(2)}) copy-start(bf16[256,128]{1,0:T(8,128)(2,1)} %constant.104.clone.first_l) | copy-start | bytes 196612
  0.0 41.6 %copy-start.14 = (bf16[256,128]{1,0:T(8,128)(2,1)S(1)}, bf16[256,128]{1,0:T(8,128)(2,1)}, u32[]{:S(2)}) copy-start(bf16[256,128]{1,0:T(8,128)(2,1)} %constant.105.clone.second_h) | copy-start | bytes 196612
  0.0 41.6 %copy-start.15 = (bf16[256,128]{1,0:T(8,128)(2,1)S(1)}, bf16[256,128]{1,0:T(8,128)(2,1)}, u32[]{:S(2)}) copy-start(bf16[256,128]{1,0:T(8,128)(2,1)} %constant.106.clone.second_l) | copy-start | bytes 196612
  45.1 38.4 %all-to-all-start.1 = ((f32[256,8,128]{2,1,0:T(8,128)}), f32[256,8,128]{2,1,0:T(8,128)S(1)}, u32[]{:S(2)}, u32[]{:S(2)}) async-start(f32[256,8,128]{2,1,0:T(8,128)} %bitcast.4), calls=%async_computation.1 | async-start | bytes 2097152 | tf_op jit(solution)/shard_map/all_to_all | solution.py:316
  53.3 0.8 copy-start.21
  54.2 0.7 copy-start.23
  55.5 0.9 copy-start.20
  56.4 27.1 %copy-start.17 = (f32[16,128]{1,0:T(8,128)S(1)}, f32[16,128]{1,0:T(8,128)}, u32[]{:S(2)}) copy-start(f32[16,128]{1,0:T(8,128)} %constant.116.clone.sin1) | copy-start | bytes 24580
  56.4 27.1 %copy-start.18 = (f32[1,1024]{1,0:T(1,128)S(1)}, f32[1,1024]{1,0:T(1,128)}, u32[]{:S(2)}) copy-start(f32[1,1024]{1,0:T(1,128)} %constant.117.clone.cos3) | copy-start | bytes 12292
  56.4 27.1 %copy-start.19 = (f32[1,1024]{1,0:T(1,128)S(1)}, f32[1,1024]{1,0:T(1,128)}, u32[]{:S(2)}) copy-start(f32[1,1024]{1,0:T(1,128)} %constant.118.clone.sin3) | copy-start | bytes 12292
  57.3 26.1 %copy-start = (f32[128,1024]{1,0:T(8,128)S(1)}, f32[128,1024]{1,0:T(8,128)}, u32[]{:S(2)}) copy-start(f32[128,1024]{1,0:T(8,128)} %constant.113.clone.cos2) | copy-start | bytes 1572868
  57.4 26.1 %copy-start.1 = (f32[128,1024]{1,0:T(8,128)S(1)}, f32[128,1024]{1,0:T(8,128)}, u32[]{:S(2)}) copy-start(f32[128,1024]{1,0:T(8,128)} %constant.114.clone.sin2) | copy-start | bytes 1572868
  57.4 26.1 %copy-start.4 = (bf16[256,256]{1,0:T(8,128)(2,1)S(1)}, bf16[256,256]{1,0:T(8,128)(2,1)}, u32[]{:S(2)}) copy-start(bf16[256,256]{1,0:T(8,128)(2,1)} %constant.109.clone.fwd_h) | copy-start | bytes 393220
  57.4 26.1 %copy-start.5 = (bf16[256,256]{1,0:T(8,128)(2,1)S(1)}, bf16[256,256]{1,0:T(8,128)(2,1)}, u32[]{:S(2)}) copy-start(bf16[256,256]{1,0:T(8,128)(2,1)} %constant.110.clone.fwd_l) | copy-start | bytes 393220
  57.4 26.1 %copy-start.6 = (bf16[256,256]{1,0:T(8,128)(2,1)S(1)}, bf16[256,256]{1,0:T(8,128)(2,1)}, u32[]{:S(2)}) copy-start(bf16[256,256]{1,0:T(8,128)(2,1)} %constant.111.clone.inv_h) | copy-start | bytes 393220
  57.4 26.1 %copy-start.7 = (bf16[256,256]{1,0:T(8,128)(2,1)S(1)}, bf16[256,256]{1,0:T(8,128)(2,1)}, u32[]{:S(2)}) copy-start(bf16[256,256]{1,0:T(8,128)(2,1)} %constant.112.clone.inv_l) | copy-start | bytes 393220
  57.4 26.1 %copy-start.16 = (f32[16,128]{1,0:T(8,128)S(1)}, f32[16,128]{1,0:T(8,128)}, u32[]{:S(2)}) copy-start(f32[16,128]{1,0:T(8,128)} %constant.115.clone.cos1) | copy-start | bytes 24580
  88.8 37.1 %copy-start.8 = (bf16[128,256]{1,0:T(8,128)(2,1)S(1)}, bf16[128,256]{1,0:T(8,128)(2,1)}, u32[]{:S(2)}) copy-start(bf16[128,256]{1,0:T(8,128)(2,1)} %constant.119.clone.first_h) | copy-start | bytes 196612
  88.8 37.1 %copy-start.9 = (bf16[128,256]{1,0:T(8,128)(2,1)S(1)}, bf16[128,256]{1,0:T(8,128)(2,1)}, u32[]{:S(2)}) copy-start(bf16[128,256]{1,0:T(8,128)(2,1)} %constant.120.clone.first_l) | copy-start | bytes 196612
  88.8 37.1 %copy-start.10 = (bf16[128,256]{1,0:T(8,128)(2,1)S(1)}, bf16[128,256]{1,0:T(8,128)(2,1)}, u32[]{:S(2)}) copy-start(bf16[128,256]{1,0:T(8,128)(2,1)} %constant.121.clone.second_h) | copy-start | bytes 196612
  88.9 37.1 %copy-start.11 = (bf16[128,256]{1,0:T(8,128)(2,1)S(1)}, bf16[128,256]{1,0:T(8,128)(2,1)}, u32[]{:S(2)}) copy-start(bf16[128,256]{1,0:T(8,128)(2,1)} %constant.122.clone.second_l) | copy-start | bytes 196612
  130.7 5.5 %copy-start.22 = (s32[1024]{0:T(1024)S(1)}, s32[1024]{0:T(1024)}, u32[]{:S(2)}) copy-start(s32[1024]{0:T(1024)} %param.32) | copy-start | bytes 12292
  130.7 5.5 %copy-start.24 = (f32[64]{0:T(128)S(1)}, f32[64]{0:T(128)}, u32[]{:S(2)}) copy-start(f32[64]{0:T(128)} %param.31) | copy-start | bytes 772
  130.7 36.4 %all-to-all-start.3 = ((f32[16,128,128]{2,1,0:T(8,128)}), f32[16,128,128]{2,1,0:T(8,128)S(1)}, u32[]{:S(2)}, u32[]{:S(2)}) async-start(f32[16,128,128]{2,1,0:T(8,128)} %bitcast.9), calls=%async_computation.3 | async-start | bytes 2097152 | tf_op jit(solution)/shard_map/all_to_all | solution.py:320
where the time goes:
time: 169 us; the launch traced here: 168 us
  blocking collectives  78.7 us (47%)
  waiting for transfers between devices  56.7 us (34%)
  starting transfers between devices  13.7 us (8%)
  Pallas kernels  13.4 us (8%)
  local copies, waits for them, and re-layouts  2.96 us (2%)
    all_to_all x1, blocking collectives, per_device(): x = lax.all_to_all(x, 'chan', 0, 0, tiled=True).reshape(2048, 128)  41.6 us
    all_to_all x1, blocking collectives, per_device(): x = lax.all_to_all(x, both, 0, 0, tiled=True).reshape(2048, 128)  37.1 us
    all_to_all x1, waiting for transfers between devices, per_device(): x = lax.all_to_all(x, 'chan', 0, 0, tiled=True)  30.7 us
    all_to_all x1, waiting for transfers between devices, per_device(): x = lax.all_to_all(x, both, 0, 0, tiled=True).reshape(2048, 128)  26 us
    pallas_call x3, Pallas kernels, call(): pl.pallas_call(body, out_shape=jax.ShapeDtypeStruct((2048, 128), f32), in...  13.4 us
    all_to_all x1, starting transfers between devices, per_device(): x = lax.all_to_all(x, both, 0, 0, tiled=True).reshape(2048, 128)  8.16 us
    all_to_all x1, starting transfers between devices, per_device(): x = lax.all_to_all(x, 'chan', 0, 0, tiled=True)  5.52 us
  transfers between devices with their start and end apart: 2, of which 2 were waited for; matrix products, arithmetic and copies ran while one was open for 1% of the time, Pallas kernels for 0%

commit v1 on v0

v1 whole, which is shorter than its diff:
```python
import math

import jax
import jax.numpy as jnp
import numpy as np
from jax import lax
from jax.experimental import pallas as pl
from jax.experimental.pallas import tpu as pltpu
from jax.sharding import PartitionSpec as P

f32 = jnp.float32
bf16 = jnp.bfloat16


def circle(product, period):
    theta = (product % period).astype(np.float64) * (2.0 * math.pi / period)
    return np.cos(theta), np.sin(theta)


def halves(table):
    table = np.asarray(table, np.float64)
    high = table.astype(np.float32).astype(jnp.bfloat16)
    low = (table - high.astype(np.float64)).astype(np.float32).astype(jnp.bfloat16)
    return high, low


def channel_tables():
    n = np.arange(128)
    cos, sin = circle(n[:, None] * n[None, :], 128)
    turn_cos, turn_sin = circle(n[:, None] * n[None, :], 16384)
    first = np.concatenate([cos, -sin], axis=0)
    second = np.zeros((2, 128, 2, 2, 32))
    for h in range(2):
        c, s = cos[:, 32 * h : 32 * h + 32], sin[:, 32 * h : 32 * h + 32]
        second[0, :, h, 0], second[1, :, h, 0] = c, s
        second[0, :, h, 1], second[1, :, h, 1] = -s, c
    second = second.reshape(256, 128)
    return first, second, turn_cos.astype(np.float32), turn_sin.astype(np.float32)


def column_f1():
    col = np.arange(1024)
    lane = col % 128
    return 4 * (col // 128) + 2 * ((lane // 32) % 2) + lane // 64


def time_tables():
    n = np.arange(128)
    cos, sin = circle(n[:, None] * n[None, :], 128)
    forward = np.block([[cos, sin], [-sin, cos]])
    f1 = column_f1()
    turn_cos, turn_sin = circle(n[:, None] * f1[None, :], 4096)
    g0 = (np.arange(128) // 32) % 2
    m = np.arange(8)
    early_cos, early_sin = circle(m[:, None] * g0[None, :], 16)
    shift_cos, shift_sin = circle(f1[None, :], 32)
    single = lambda *arrays: [np.asarray(a, np.float32) for a in arrays]
    return forward, single(turn_cos, turn_sin, early_cos, early_sin, shift_cos, shift_sin)


def split(x):
    high = x.astype(bf16)
    return high, (x - high.astype(f32)).astype(bf16)


def mm(a, b):
    return jnp.dot(a, b, preferred_element_type=f32)


def left_table(table):
    high, low = halves(table)
    return np.concatenate([high, high, low], axis=1)


def right_table(table):
    high, low = halves(table)
    return np.concatenate([high, high, low], axis=0)


def left(table, x):
    high, low = split(x)
    return mm(table, jnp.concatenate([high, low, high], axis=0))


def right(x, table):
    high, low = split(x)
    return mm(jnp.concatenate([high, low, high], axis=1), table)


def lane_bit(rows, bit):
    lane = lax.broadcasted_iota(jnp.int32, (rows, 128), 1)
    return (lane & bit) != 0


def exchange(a, b, mask, bit):
    rolled_b = pltpu.roll(b, bit, 1)
    rolled_a = pltpu.roll(a, 128 - bit, 1)
    return jnp.where(mask, rolled_b, a), jnp.where(mask, b, rolled_a)


def rotate(re, im, angle_num, angle_den, sign):
    num = (angle_num * 8) / angle_den
    if num == 0:
        return re, im
    if num == 2:
        return (im, -re) if sign < 0 else (-im, re)
    if num == 1 or num == 3:
        root = math.sqrt(0.5)
        if sign < 0:
            a, b = (re + im, im - re) if num == 1 else (im - re, -re - im)
        else:
            a, b = (re - im, im + re) if num == 1 else (-re - im, re - im)
        return a * root, b * root
    c = math.cos(2 * math.pi * angle_num / angle_den)
    s = sign * math.sin(2 * math.pi * angle_num / angle_den)
    return re * c - im * s, im * c + re * s


def small_fft(re, im, sign):
    n = len(re)
    if n == 1:
        return re, im
    er, ei = small_fft(re[0::2], im[0::2], sign)
    odd_r, odd_i = small_fft(re[1::2], im[1::2], sign)
    out_r, out_i = [None] * n, [None] * n
    for k in range(n // 2):
        tr, ti = rotate(odd_r[k], odd_i[k], k, n, sign)
        out_r[k], out_i[k] = er[k] + tr, ei[k] + ti
        out_r[k + n // 2], out_i[k + n // 2] = er[k] - tr, ei[k] - ti
    return out_r, out_i


def turned_tables(cos, sin, phase, cos_b, sin_b):
    pc, ps = phase[0:1, :], phase[1:2, :]
    cos_b[...] = cos[...] * pc - sin[...] * ps
    sin_b[...] = sin[...] * pc + cos[...] * ps


def channel_forward(x, first, second, cos, sin, phase, out, cos_b, sin_b):
    turned_tables(cos, sin, phase, cos_b, sin_b)
    mask = lane_bit(128, 64)
    for rl in range(8):
        early = x[pl.ds(rl, 128, stride=8), :]
        late = x[pl.ds(1024 + rl, 128, stride=8), :]
        y = left(first[...], jnp.concatenate([early + late, early - late], axis=1))
        turned = []
        for f0, (c, s) in enumerate(((cos[...], sin[...]), (cos_b[...], sin_b[...]))):
            yr = y[:128, 128 * f0 : 128 * f0 + 128]
            yi = y[128:, 128 * f0 : 128 * f0 + 128]
            turned.append(jnp.concatenate([yr * c + yi * s, yi * c - yr * s], axis=1))
        o = right(jnp.concatenate(turned, axis=0), second[...])
        low, high = exchange(o[:128], o[128:], mask, 64)
        out[pl.ds(rl, 128, stride=16), :] = low
        out[pl.ds(8 + rl, 128, stride=16), :] = high


def channel_inverse(x, first, second, cos, sin, phase, out, cos_b, sin_b):
    turned_tables(cos, sin, phase, cos_b, sin_b)
    mask = lane_bit(128, 64)
    for rl in range(8):
        low = x[pl.ds(rl, 128, stride=16), :]
        high = x[pl.ds(8 + rl, 128, stride=16), :]
        u = right(jnp.concatenate(exchange(low, high, mask, 64), axis=0), second[...])
        turned = []
        for f0, (c, s) in enumerate(((cos[...], sin[...]), (cos_b[...], sin_b[...]))):
            ur = u[128 * f0 : 128 * f0 + 128, :128]
            ui = u[128 * f0 : 128 * f0 + 128, 128:]
            turned.append(jnp.concatenate([ur * c - ui * s, ui * c + ur * s], axis=0))
        o = left(first[...], jnp.concatenate(turned, axis=1))
        out[pl.ds(rl, 128, stride=8), :] = o[:, :128] + o[:, 128:]
        out[pl.ds(1024 + rl, 128, stride=8), :] = o[:, :128] - o[:, 128:]


def tile_row(m, tile):
    return 8 * (128 * (m % 2) + 16 * (m // 2) + tile)


def time_part(
    x, factor, fir, fwd, inv, cos2, sin2, cos1, sin1, cos3, sin3, out, work, past, future
):
    bit32, bit64 = lane_bit(8, 32), lane_bit(8, 64)
    for tile in range(16):
        rows = [tile_row(m, tile) for m in range(16)]
        values = [x[row : row + 8, :] for row in rows]
        re, im = [], []
        for m in range(8):
            r, i = exchange(values[m] + values[m + 8], values[m] - values[m + 8], bit32, 32)
            if m > 0:
                c, s = cos1[m : m + 1, :], sin1[m : m + 1, :]
                r, i = r * c + i * s, i * c - r * s
            re.append(r)
            im.append(i)
        re, im = small_fft(re, im, -1)
        for g in range(8):
            work[tile * 8 : tile * 8 + 8, g * 128 : g * 128 + 128] = re[g]
            work[128 + tile * 8 : 136 + tile * 8, g * 128 : g * 128 + 128] = im[g]

    fir_high, fir_low = split(fir[...])
    fir_table = jnp.concatenate([fir_high, fir_high, fir_low], axis=1)
    for step in range(4):
        cols = slice(256 * step, 256 * step + 256)
        c, s = cos2[:, cols], sin2[:, cols]
        re, im = work[:128, cols], work[128:, cols]
        b = jnp.concatenate([re * c + im * s, im * c - re * s], axis=0)
        spectrum = left(fwd[...], b)
        kept = factor[:, cols]
        spectrum = jnp.concatenate([spectrum[:128] * kept, spectrum[128:] * kept], axis=0)
        z = left(inv[...], spectrum)
        re, im = z[:128], z[128:]
        v = left(fir_table, jnp.concatenate([re * c - im * s, im * c + re * s], axis=1))
        same, before, after = v[:128], v[128:256], v[256:]
        total, differ = before + after, after - before
        c, s = cos3[:, cols], sin3[:, cols]
        work[:128, cols] = same[:, :256] + (total[:, :256] * c - differ[:, 256:] * s)
        work[128:, cols] = same[:, 256:] + (total[:, 256:] * c + differ[:, :256] * s)
        br, bi = before[:, :256], before[:, 256:]
        wr, wi = br * c + bi * s, bi * c - br * s
        wrapped = jnp.concatenate([wr[:, :128] + wr[:, 128:], wi[:, :128] + wi[:, 128:]], axis=1)
        ahead = jnp.concatenate(
            [after[:, :128] + after[:, 128:256], after[:, 256:384] + after[:, 384:]], axis=1
        )
        if step == 0:
            past[...] = wrapped
            future[...] = ahead
        else:
            past[...] += wrapped
            future[...] += ahead

    last_c, last_s = math.cos(2 * math.pi * 15 / 32), math.sin(2 * math.pi * 15 / 32)
    for tile in range(16):
        rows = slice(tile * 8, tile * 8 + 8)
        below = slice(128 + tile * 8, 136 + tile * 8)
        re = [work[rows, g * 128 : g * 128 + 128] for g in range(8)]
        im = [work[below, g * 128 : g * 128 + 128] for g in range(8)]
        re, im = small_fft(re, im, 1)
        sums = []
        for ref in (past, future):
            for part in range(2):
                e = ref[rows, part * 128 : part * 128 + 128] * 0.5
                e = e + pltpu.roll(e, 64, 1)
                sums.append(e + pltpu.roll(e, 32, 1))
        first_edge = jnp.where(bit32, sums[1], sums[0])
        turned_re = sums[2] * last_c + sums[3] * last_s
        turned_im = sums[3] * last_c - sums[2] * last_s
        last_edge = jnp.where(
            bit64, -jnp.where(bit32, turned_im, turned_re), jnp.where(bit32, sums[3], sums[2])
        )
        for m in range(8):
            r, i = re[m], im[m]
            if m > 0:
                c, s = cos1[m : m + 1, :], sin1[m : m + 1, :]
                r, i = r * c - i * s, i * c + r * s
            even, odd = exchange(r, i, bit32, 32)
            low, high = even + odd, even - odd
            if m == 0:
                low = low - first_edge
            if m == 7:
                high = high - last_edge
            row = tile_row(m, tile)
            out[row : row + 8, :] = low
            row = tile_row(m + 8, tile)
            out[row : row + 8, :] = high


def call(body, args, scratch=()):
    return pl.pallas_call(
        body,
        out_shape=jax.ShapeDtypeStruct((2048, 128), f32),
        in_specs=[pl.BlockSpec(memory_space=pltpu.VMEM)] * len(args),
        out_specs=pl.BlockSpec(memory_space=pltpu.VMEM),
        scratch_shapes=list(scratch),
        compiler_params=pltpu.CompilerParams(vmem_limit_bytes=40 * 1024 * 1024),
        name=body.__name__,
    )(*args)


def forward_kernel(x, phase):
    first, second, cos, sin = channel_tables()
    scratch = [pltpu.VMEM((128, 128), f32)] * 2
    return call(
        channel_forward, (x, left_table(first), right_table(second), cos, sin, phase), scratch
    )


def inverse_kernel(x, phase):
    first, second, cos, sin = channel_tables()
    scratch = [pltpu.VMEM((128, 128), f32)] * 2
    return call(
        channel_inverse, (x, left_table(first.T), right_table(second.T), cos, sin, phase), scratch
    )


def time_kernel(x, factor, fir):
    forward, tables = time_tables()
    args = (x, factor, fir, left_table(forward), left_table(forward.T), *tables)
    scratch = (
        pltpu.VMEM((256, 1024), f32),
        pltpu.VMEM((128, 256), f32),
        pltpu.VMEM((128, 256), f32),
    )
    return call(time_part, args, scratch)


def fir_matrix(taps):
    padded = jnp.concatenate([jnp.zeros((1,), f32), taps, jnp.zeros((129,), f32)])
    wide = jnp.tile(padded, 128)[: 128 * 384].reshape(128, 384)
    return jnp.concatenate([wide[:, 128:256], wide[:, :128], wide[:, 256:]], axis=0)


def mask_factor(band_edges, owner, scale):
    spread = (np.arange(32)[:, None] == column_f1()[None, :]).astype(np.float32)
    edges = band_edges.astype(f32).reshape(256, 32)
    edges = jnp.dot(edges, spread, precision=lax.Precision.HIGHEST)
    kl = jnp.arange(1024, dtype=jnp.int32) % 32
    wave = owner // 2 + 128 * (32 * (owner % 2) + kl)
    wave_f = wave.astype(f32)[None, :]
    kept = (wave_f >= edges[:128]) & (wave_f <= edges[128:])
    weight = jnp.where(wave == 0, scale, 2.0 * scale).astype(f32)[None, :]
    return jnp.where(kept, weight, 0.0)


def device_phase():
    tm = lax.axis_index("tm")
    m = 2 * (tm & 7) + (tm >> 3)
    table = np.stack(circle(np.arange(16), 32), axis=1).astype(np.float32)
    table = np.repeat(table[:, :, None], 128, axis=2)
    return lax.dynamic_index_in_dim(jnp.asarray(table), m, 0, keepdims=False)


def per_device(traces, band_edges, taps, gain_table, gain_index):
    both = ("tm", "chan")
    groups = [[16 * (8 * i + t) + c for i in range(2) for c in range(16)] for t in range(8)]
    owner = lax.axis_index("tm") * 16 + lax.axis_index("chan")
    factor = mask_factor(band_edges, owner, 1.0 / (4096 * 16384))
    fir = fir_matrix(taps)
    phase = device_phase()
    matches = gain_index[:, None] == jnp.arange(64, dtype=jnp.int32)[None, :]
    gains = jnp.sum(jnp.where(matches, gain_table[None, :], 0.0), axis=1)

    x = traces.reshape(32, 8, 8, 128).transpose(0, 2, 1, 3).reshape(32, 64, 128)
    x = lax.all_to_all(x, both, 0, 0, tiled=True, axis_index_groups=groups).reshape(2048, 128)
    x = forward_kernel(x, phase).reshape(256, 8, 128)
    x = lax.all_to_all(x, both, 0, 0, tiled=True).reshape(2048, 128)
    x = time_kernel(x, factor, fir).reshape(256, 8, 128)
    x = lax.all_to_all(x, both, 0, 0, tiled=True).reshape(2048, 128)
    x = inverse_kernel(x, phase).reshape(32, 64, 128)
    x = lax.all_to_all(x, both, 0, 0, tiled=True, axis_index_groups=groups)
    x = x.reshape(32, 8, 8, 128).transpose(0, 2, 1, 3).reshape(256, 1024)
    return x * gains[None, :]


def solution(mesh):
    in_specs = (P("tm", "chan"), P(), P(), P(), P("chan"))
    return jax.shard_map(
        per_device, mesh=mesh, in_specs=in_specs, out_specs=P("tm", "chan"), check_vma=False
    )
```

time: 169 us -> 168 us (level)
  blocking collectives: 78.7 us -> 37.1 us
  waiting for transfers between devices: 56.7 us -> 86.1 us
  starting transfers between devices: 13.7 us -> 23.5 us
    all_to_all x1 -> x0, blocking collectives: 41.6 us -> none  [per_device(): x = lax.all_to_all(x, 'chan', 0, 0, tiled=True).reshape(2048, 128)]
    all_to_all x1 -> x2, waiting for transfers between devices: 30.7 us -> 60.2 us  [the longest x1 30.2 us: per_device(): lax.all_to_all(x, both, 0, 0, tiled=True, axis_index_groups=groups)]
    all_to_all x1 -> x2, starting transfers between devices: 5.52 us -> 16.8 us  [the longest x1 11.2 us: per_device(): lax.all_to_all(x, both, 0, 0, tiled=True, axis_index_groups=groups)]
  transfers between devices with their start and end apart: 2 -> 3, of which waited for: 2 -> 3; matrix products, arithmetic and copies ran while one was open for 1% -> 2% of each run, Pallas kernels for 0% -> 0%
where the time goes in v1:
time: 168 us; the launch traced here: 167 us
  waiting for transfers between devices  86.1 us (51%)
  blocking collectives  37.1 us (22%)
  starting transfers between devices  23.5 us (14%)
  Pallas kernels  13.4 us (8%)
  local copies, waits for them, and re-layouts  4.59 us (3%)
    all_to_all x1, blocking collectives, per_device(): x = lax.all_to_all(x, both, 0, 0, tiled=True).reshape(2048, 128)  37.1 us
    all_to_all x1, waiting for transfers between devices, per_device(): lax.all_to_all(x, both, 0, 0, tiled=True, axis_index_groups=groups)  30.2 us
    all_to_all x1, waiting for transfers between devices, per_device(): x = lax.all_to_all(x, both, 0, 0, tiled=True, axis_index_groups=groups)  30 us
    all_to_all x1, waiting for transfers between devices, per_device(): x = lax.all_to_all(x, both, 0, 0, tiled=True).reshape(2048, 128)  26 us
    pallas_call x3, Pallas kernels, call(): pl.pallas_call(body, out_shape=jax.ShapeDtypeStruct((2048, 128), f32), in...  13.4 us
    all_to_all x1, starting transfers between devices, per_device(): lax.all_to_all(x, both, 0, 0, tiled=True, axis_index_groups=groups)  11.2 us
    all_to_all x1, starting transfers between devices, per_device(): x = lax.all_to_all(x, both, 0, 0, tiled=True).reshape(2048, 128)  6.64 us
    all_to_all x1, starting transfers between devices, per_device(): x = lax.all_to_all(x, both, 0, 0, tiled=True, axis_index_groups=groups)  5.66 us
  transfers between devices with their start and end apart: 3, of which 3 were waited for; matrix products, arithmetic and copies ran while one was open for 2% of the time, Pallas kernels for 0%

profile of v1, /device:TPU:33, one launch (start us, length us, event | category | flops | bytes accessed | tf_op | source)
XLA Modules:
  0.0 167.4 jit_solution(4667069934293506147)
XLA Ops:
  0.0 0.0 copy-start.9
  0.0 11.2 %all-to-all-start = ((f32[32,64,128]{2,1,0:T(8,128)}), f32[32,64,128]{2,1,0:T(8,128)S(1)}, u32[]{:S(2)}, u32[]{:S(2)}) async-start(f32[32,64,128]{2,1,0:T(8,128)} %bitcast.27), calls=%async_computation | async-start | bytes 2097152 | tf_op jit(solution)/shard_map/all_to_all | solution.py:341
  11.2 0.7 dynamic-slice_bitcast_fusion.phase
  11.9 30.2 %all-to-all-done = f32[32,64,128]{2,1,0:T(8,128)S(1)} async-done(((f32[32,64,128]{2,1,0:T(8,128)}), f32[32,64,128]{2,1,0:T(8,128)S(1)}, u32[]{:S(2)}, u32[]{:S(2)}) %all-to-all-start) | async-done | bytes 1048608 | tf_op jit(solution)/shard_map/all_to_all | solution.py:341
  42.0 0.0 copy-done.4
  42.1 0.0 copy-done.5
  42.1 0.0 copy-done.8
  42.1 0.0 copy-done.9
  42.1 4.2 %channel_forward.1 = f32[2048,128]{1,0:T(8,128)} custom-call(f32[2048,128]{1,0:T(8,128)S(1)} %bitcast.23, bf16[256,384]{1,0:T(8,128)(2,1)S(1)} %copy-done.8, bf16[768,128]{1,0:T(8,128)(2,1)S(1)} %copy-done.9, f32[128,128]{1,0:T(8,128)S(1)} %copy-done.4, f32[128,128]{1,0:T(8,128)S(1)} %copy-done.5, f32[2,128]{1,0:T(2,128)S(1)} %dynamic-slice_bitcast_fusion.phase), custom_call_target="tpu_custom_call" | custom-call | tf_op jit(solution)/shard_map/channel_forward/pallas_call | solution.py:266
  46.3 6.6 %all-to-all-start.1 = ((f32[256,8,128]{2,1,0:T(8,128)}), f32[256,8,128]{2,1,0:T(8,128)S(1)}, u32[]{:S(2)}, u32[]{:S(2)}) async-start(f32[256,8,128]{2,1,0:T(8,128)} %bitcast.5), calls=%async_computation.1 | async-start | bytes 2097152 | tf_op jit(solution)/shard_map/all_to_all | solution.py:343
  52.9 0.0 copy-start.15
  53.0 0.7 copy-done.15
  53.7 0.1 reshape.62
  53.8 0.0 copy-start.17
  53.9 0.7 copy-done.17
  54.5 0.1 pad_maximum_fusion.1
  54.6 0.3 tile.10
  55.1 0.0 copy-start.14
  55.2 0.9 copy-done.14
  56.0 1.0 convolution_bitcast_fusion
  57.0 0.0 copy-start
  57.0 0.0 copy-start.1
  57.0 0.0 copy-start.2
  57.0 0.0 copy-start.10
  57.0 0.0 copy-start.11
  57.1 0.0 copy-start.12
  57.1 0.0 copy-start.13
  57.1 0.1 fusion.1.factor
  57.2 26.0 %all-to-all-done.1 = f32[256,8,128]{2,1,0:T(8,128)S(1)} async-done(((f32[256,8,128]{2,1,0:T(8,128)}), f32[256,8,128]{2,1,0:T(8,128)S(1)}, u32[]{:S(2)}, u32[]{:S(2)}) %all-to-all-start.1) | async-done | bytes 1048608 | tf_op jit(solution)/shard_map/all_to_all | solution.py:343
  83.2 0.0 copy-done
  83.2 0.0 copy-done.1
  83.2 0.0 copy-done.2
  83.2 0.0 copy-done.10
  83.2 0.0 copy-done.11
  83.2 0.0 copy-done.12
  83.2 0.0 copy-start.3
  83.2 1.0 copy-done.3
  84.2 4.9 %time_part.1 = f32[2048,128]{1,0:T(8,128)S(1)} custom-call(f32[2048,128]{1,0:T(8,128)S(1)} %bitcast.25, f32[128,1024]{1,0:T(8,128)S(1)} %fusion.1.factor, f32[384,128]{1,0:T(8,128)S(1)} %pad_maximum_fusion.fir, bf16[256,768]{1,0:T(8,128)(2,1)S(1)} %copy-done.2, bf16[256,768]{1,0:T(8,128)(2,1)S(1)} %copy-done.3, f32[128,1024]{1,0:T(8,128)S(1)} %copy-done, ...), custom_call_target="tpu_custom_call" | custom-call | tf_op jit(solution)/shard_map/time_part/pallas_call | solution.py:266
  89.1 0.0 copy-start.6
  89.1 0.0 copy-start.7
  89.1 37.1 %all_to_all.20 = f32[256,8,128]{2,1,0:T(8,128)S(1)} all-to-all(f32[256,8,128]{2,1,0:T(8,128)S(1)} %bitcast.26), channel_id=1, replica_groups=mesh['tm'=16,'chan'=16] {'tm','chan'}, dimensions={0} | all-to-all | bytes 2097152 | tf_op jit(solution)/shard_map/all_to_all | solution.py:345
  126.2 4.3 %channel_inverse.1 = f32[2048,128]{1,0:T(8,128)} custom-call(f32[2048,128]{1,0:T(8,128)S(1)} %bitcast.24, bf16[128,768]{1,0:T(8,128)(2,1)S(1)} %copy-done.6, bf16[384,256]{1,0:T(8,128)(2,1)S(1)} %copy-done.7, f32[128,128]{1,0:T(8,128)S(1)} %copy-done.4, f32[128,128]{1,0:T(8,128)S(1)} %copy-done.5, f32[2,128]{1,0:T(2,128)S(1)} %dynamic-slice_bitcast_fusion.phase), custom_call_target="tpu_custom_call" | custom-call | tf_op jit(solution)/shard_map/channel_inverse/pallas_call | solution.py:266
  130.5 5.7 %all-to-all-start.3 = ((f32[32,64,128]{2,1,0:T(8,128)}), f32[32,64,128]{2,1,0:T(8,128)S(1)}, u32[]{:S(2)}, u32[]{:S(2)}) async-start(f32[32,64,128]{2,1,0:T(8,128)} %bitcast.10), calls=%async_computation.3 | async-start | bytes 2097152 | tf_op jit(solution)/shard_map/all_to_all | solution.py:347
  136.1 0.0 copy-done.16
  136.2 0.0 copy-done.18
  136.2 0.1 select_reduce_fusion
  136.3 30.0 %all-to-all-done.3 = f32[32,64,128]{2,1,0:T(8,128)S(1)} async-done(((f32[32,64,128]{2,1,0:T(8,128)}), f32[32,64,128]{2,1,0:T(8,128)S(1)}, u32[]{:S(2)}, u32[]{:S(2)}) %all-to-all-start.3) | async-done | bytes 1048608 | tf_op jit(solution)/shard_map/all_to_all | solution.py:347
  166.3 1.1 bitcast_multiply_fusion
  (17 shorter events, 0.2 us)
Async XLA Ops:
  0.0 42.1 %copy-start.4 = (f32[128,128]{1,0:T(8,128)S(1)}, f32[128,128]{1,0:T(8,128)}, u32[]{:S(2)}) copy-start(f32[128,128]{1,0:T(8,128)} %constant.104.clone.cos) | copy-start | bytes 196612
  0.0 42.1 %copy-start.5 = (f32[128,128]{1,0:T(8,128)S(1)}, f32[128,128]{1,0:T(8,128)}, u32[]{:S(2)}) copy-start(f32[128,128]{1,0:T(8,128)} %constant.105.clone.sin) | copy-start | bytes 196612
  0.0 42.1 %copy-start.8 = (bf16[256,384]{1,0:T(8,128)(2,1)S(1)}, bf16[256,384]{1,0:T(8,128)(2,1)}, u32[]{:S(2)}) copy-start(bf16[256,384]{1,0:T(8,128)(2,1)} %constant.102.clone.first) | copy-start | bytes 589828
  0.0 42.1 %copy-start.9 = (bf16[768,128]{1,0:T(8,128)(2,1)S(1)}, bf16[768,128]{1,0:T(8,128)(2,1)}, u32[]{:S(2)}) copy-start(bf16[768,128]{1,0:T(8,128)(2,1)} %constant.103.clone.second) | copy-start | bytes 589828
  0.0 42.0 %all-to-all-start = ((f32[32,64,128]{2,1,0:T(8,128)}), f32[32,64,128]{2,1,0:T(8,128)S(1)}, u32[]{:S(2)}, u32[]{:S(2)}) async-start(f32[32,64,128]{2,1,0:T(8,128)} %bitcast.27), calls=%async_computation | async-start | bytes 2097152 | tf_op jit(solution)/shard_map/all_to_all | solution.py:341
  46.3 36.9 %all-to-all-start.1 = ((f32[256,8,128]{2,1,0:T(8,128)}), f32[256,8,128]{2,1,0:T(8,128)S(1)}, u32[]{:S(2)}, u32[]{:S(2)}) async-start(f32[256,8,128]{2,1,0:T(8,128)} %bitcast.5), calls=%async_computation.1 | async-start | bytes 2097152 | tf_op jit(solution)/shard_map/all_to_all | solution.py:343
  52.9 0.8 copy-start.15
  53.8 0.7 copy-start.17
  55.1 0.9 copy-start.14
  57.0 26.2 %copy-start = (f32[128,1024]{1,0:T(8,128)S(1)}, f32[128,1024]{1,0:T(8,128)}, u32[]{:S(2)}) copy-start(f32[128,1024]{1,0:T(8,128)} %constant.108.clone.cos2) | copy-start | bytes 1572868
  57.0 26.1 %copy-start.1 = (f32[128,1024]{1,0:T(8,128)S(1)}, f32[128,1024]{1,0:T(8,128)}, u32[]{:S(2)}) copy-start(f32[128,1024]{1,0:T(8,128)} %constant.109.clone.sin2) | copy-start | bytes 1572868
  57.0 26.1 %copy-start.2 = (bf16[256,768]{1,0:T(8,128)(2,1)S(1)}, bf16[256,768]{1,0:T(8,128)(2,1)}, u32[]{:S(2)}) copy-start(bf16[256,768]{1,0:T(8,128)(2,1)} %constant.106.clone.fwd) | copy-start | bytes 1179652
  57.0 26.1 %copy-start.10 = (f32[8,128]{1,0:T(8,128)S(1)}, f32[8,128]{1,0:T(8,128)}, u32[]{:S(2)}) copy-start(f32[8,128]{1,0:T(8,128)} %constant.110.clone.cos1) | copy-start | bytes 12292
  57.0 26.1 %copy-start.11 = (f32[8,128]{1,0:T(8,128)S(1)}, f32[8,128]{1,0:T(8,128)}, u32[]{:S(2)}) copy-start(f32[8,128]{1,0:T(8,128)} %constant.111.clone.sin1) | copy-start | bytes 12292
  57.1 26.1 %copy-start.12 = (f32[1,1024]{1,0:T(1,128)S(1)}, f32[1,1024]{1,0:T(1,128)}, u32[]{:S(2)}) copy-start(f32[1,1024]{1,0:T(1,128)} %constant.112.clone.cos3) | copy-start | bytes 12292
  57.1 26.1 %copy-start.13 = (f32[1,1024]{1,0:T(1,128)S(1)}, f32[1,1024]{1,0:T(1,128)}, u32[]{:S(2)}) copy-start(f32[1,1024]{1,0:T(1,128)} %constant.113.clone.sin3) | copy-start | bytes 12292
  83.2 1.0 copy-start.3
  89.1 37.1 %copy-start.6 = (bf16[128,768]{1,0:T(8,128)(2,1)S(1)}, bf16[128,768]{1,0:T(8,128)(2,1)}, u32[]{:S(2)}) copy-start(bf16[128,768]{1,0:T(8,128)(2,1)} %constant.114.clone.first) | copy-start | bytes 589828
  89.1 37.1 %copy-start.7 = (bf16[384,256]{1,0:T(8,128)(2,1)S(1)}, bf16[384,256]{1,0:T(8,128)(2,1)}, u32[]{:S(2)}) copy-start(bf16[384,256]{1,0:T(8,128)(2,1)} %constant.115.clone.second) | copy-start | bytes 589828
  130.5 5.7 %copy-start.16 = (s32[1024]{0:T(1024)S(1)}, s32[1024]{0:T(1024)}, u32[]{:S(2)}) copy-start(s32[1024]{0:T(1024)} %param.27) | copy-start | bytes 12292
  130.5 5.7 %copy-start.18 = (f32[64]{0:T(128)S(1)}, f32[64]{0:T(128)}, u32[]{:S(2)}) copy-start(f32[64]{0:T(128)} %param.26) | copy-start | bytes 772
  130.5 35.8 %all-to-all-start.3 = ((f32[32,64,128]{2,1,0:T(8,128)}), f32[32,64,128]{2,1,0:T(8,128)S(1)}, u32[]{:S(2)}, u32[]{:S(2)}) async-start(f32[32,64,128]{2,1,0:T(8,128)} %bitcast.10), calls=%async_computation.3 | async-start | bytes 2097152 | tf_op jit(solution)/shard_map/all_to_all | solution.py:347

commit v2 on v1

--- a/solution.py
+++ b/solution.py
@@ -80,6 +80,26 @@
 def left(table, x):
     high, low = split(x)
     return mm(table, jnp.concatenate([high, low, high], axis=0))
+
+
+def left_apart(table, x):
+    high, low = split(x)
+    k = x.shape[0]
+    return mm(table[:, :k], high) + (mm(table[:, :k], low) + mm(table[:, 2 * k :], high))
+
+
+def left_pair(table, x):
+    high, low = split(x)
+    k = x.shape[0]
+    both = jnp.concatenate([high, low], axis=0)
+    return mm(table[:, : 2 * k], both) + mm(table[:, 2 * k :], high)
+
+
+def right_pair(x, table):
+    high, low = split(x)
+    k = x.shape[1]
+    both = jnp.concatenate([high, low], axis=1)
+    return mm(both, table[: 2 * k]) + mm(high, table[2 * k :])
 
 
 def right(x, table):
@@ -142,7 +162,7 @@
     for rl in range(8):
         early = x[pl.ds(rl, 128, stride=8), :]
         late = x[pl.ds(1024 + rl, 128, stride=8), :]
-        y = left(first[...], jnp.concatenate([early + late, early - late], axis=1))
+        y = left_apart(first[...], jnp.concatenate([early + late, early - late], axis=1))
         turned = []
         for f0, (c, s) in enumerate(((cos[...], sin[...]), (cos_b[...], sin_b[...]))):
             yr = y[:128, 128 * f0 : 128 * f0 + 128]
@@ -160,13 +180,13 @@
     for rl in range(8):
         low = x[pl.ds(rl, 128, stride=16), :]
         high = x[pl.ds(8 + rl, 128, stride=16), :]
-        u = right(jnp.concatenate(exchange(low, high, mask, 64), axis=0), second[...])
+        u = right_pair(jnp.concatenate(exchange(low, high, mask, 64), axis=0), second[...])
         turned = []
         for f0, (c, s) in enumerate(((cos[...], sin[...]), (cos_b[...], sin_b[...]))):
             ur = u[128 * f0 : 128 * f0 + 128, :128]
             ui = u[128 * f0 : 128 * f0 + 128, 128:]
             turned.append(jnp.concatenate([ur * c - ui * s, ui * c + ur * s], axis=0))
-        o = left(first[...], jnp.concatenate(turned, axis=1))
+        o = left_pair(first[...], jnp.concatenate(turned, axis=1))
         out[pl.ds(rl, 128, stride=8), :] = o[:, :128] + o[:, 128:]
         out[pl.ds(1024 + rl, 128, stride=8), :] = o[:, :128] - o[:, 128:]
 
@@ -339,6 +359,7 @@
 
     x = traces.reshape(32, 8, 8, 128).transpose(0, 2, 1, 3).reshape(32, 64, 128)
     x = lax.all_to_all(x, both, 0, 0, tiled=True, axis_index_groups=groups).reshape(2048, 128)
+    x, factor, fir, phase, gains = lax.optimization_barrier((x, factor, fir, phase, gains))
     x = forward_kernel(x, phase).reshape(256, 8, 128)
     x = lax.all_to_all(x, both, 0, 0, tiled=True).reshape(2048, 128)
     x = time_kernel(x, factor, fir).reshape(256, 8, 128)

time: 168 us -> 163 us (0.970)
  blocking collectives: 37.1 us -> 109 us
  waiting for transfers between devices: 86.1 us -> 25.9 us
  starting transfers between devices: 23.5 us -> 11 us
  Pallas kernels: 13.4 us -> 10.6 us
    all_to_all x2 -> x0, waiting for transfers between devices: 56 us -> none  [the longest x1 30 us: per_device(): x = lax.all_to_all(x, both, 0, 0, tiled=True, axis_index_groups=groups)]
    all_to_all x1 -> x2, blocking collectives: 37.1 us -> 73.8 us  [per_device(): x = lax.all_to_all(x, both, 0, 0, tiled=True).reshape(2048, 128)]
    all_to_all x0 -> x1, blocking collectives: none -> 35.5 us  [per_device(): x = lax.all_to_all(x, both, 0, 0, tiled=True, axis_index_groups=groups)]
    all_to_all x2 -> x0, starting transfers between devices: 12.3 us -> none  [the longest x1 6.64 us: per_device(): x = lax.all_to_all(x, both, 0, 0, tiled=True).reshape(2048, 128)]
    all_to_all x1, waiting for transfers between devices: 30.2 us -> 25.9 us  [per_device(): lax.all_to_all(x, both, 0, 0, tiled=True, axis_index_groups=groups)]
    pallas_call x3, Pallas kernels: 13.4 us -> 10.6 us  [call(): pl.pallas_call(body, out_shape=jax.ShapeDtypeStruct((2048, 128), f32), in...]
  transfers between devices with their start and end apart: 3 -> 1, of which waited for: 3 -> 1; matrix products, arithmetic and copies ran while one was open for 2% -> 2% of each run, Pallas kernels for 0% -> 0%
where the time goes in v2:
time: 163 us
  blocking collectives  109 us (67%)
  waiting for transfers between devices  25.9 us (16%)
  starting transfers between devices  11 us (7%)
  Pallas kernels  10.6 us (7%)
  local copies, waits for them, and re-layouts  3.52 us (2%)
    all_to_all x2, blocking collectives, per_device(): x = lax.all_to_all(x, both, 0, 0, tiled=True).reshape(2048, 128)  73.8 us
    all_to_all x1, blocking collectives, per_device(): x = lax.all_to_all(x, both, 0, 0, tiled=True, axis_index_groups=groups)  35.5 us
    all_to_all x1, waiting for transfers between devices, per_device(): lax.all_to_all(x, both, 0, 0, tiled=True, axis_index_groups=groups)  25.9 us
    all_to_all x1, starting transfers between devices, per_device(): lax.all_to_all(x, both, 0, 0, tiled=True, axis_index_groups=groups)  11 us
    pallas_call x3, Pallas kernels, call(): pl.pallas_call(body, out_shape=jax.ShapeDtypeStruct((2048, 128), f32), in...  10.6 us
  transfers between devices with their start and end apart: 1, of which 1 were waited for; matrix products, arithmetic and copies ran while one was open for 2% of the time, Pallas kernels for 0%

profile of v2, /device:TPU:33, one launch (start us, length us, event | category | flops | bytes accessed | tf_op | source)
XLA Modules:
  0.0 163.0 jit_solution(11832981547414889562)
XLA Ops:
  0.0 11.0 %all-to-all-start = ((f32[32,64,128]{2,1,0:T(8,128)}), f32[32,64,128]{2,1,0:T(8,128)S(1)}, u32[]{:S(2)}, u32[]{:S(2)}) async-start(f32[32,64,128]{2,1,0:T(8,128)} %bitcast.29), calls=%async_computation | async-start | bytes 2097152 | tf_op jit(solution)/shard_map/all_to_all | solution.py:361
  11.0 0.0 copy-start.15
  11.1 0.7 copy-done.15
  11.8 0.1 reshape.60
  11.9 0.0 copy-start.17
  12.0 0.7 copy-done.17
  12.6 0.1 pad_maximum_fusion.1
  12.7 0.3 tile.10
  13.2 0.7 dynamic-slice_bitcast_fusion.phase
  13.9 0.0 copy-start.16
  13.9 0.0 copy-start.18
  13.9 0.0 copy-start.14
  13.9 0.6 copy-done.16
  14.6 0.0 copy-done.18
  14.6 0.1 select_reduce_fusion
  14.7 0.1 copy-done.14
  14.8 1.0 convolution_bitcast_fusion
  15.8 0.0 copy-start.4
  15.8 0.0 copy-start.5
  15.8 0.0 copy-start.8
  15.8 0.0 copy-start.9
  15.9 0.1 fusion.1.factor
  15.9 25.9 %all-to-all-done = f32[32,64,128]{2,1,0:T(8,128)S(1)} async-done(((f32[32,64,128]{2,1,0:T(8,128)}), f32[32,64,128]{2,1,0:T(8,128)S(1)}, u32[]{:S(2)}, u32[]{:S(2)}) %all-to-all-start) | async-done | bytes 1048608 | tf_op jit(solution)/shard_map/all_to_all | solution.py:361
  41.9 0.0 copy-done.4
  41.9 0.0 copy-done.5
  41.9 0.0 copy-done.8
  41.9 0.0 copy-done.9
  41.9 2.5 %channel_forward.1 = f32[2048,128]{1,0:T(8,128)S(1)} custom-call(f32[2048,128]{1,0:T(8,128)S(1)} %bitcast.23, bf16[256,384]{1,0:T(8,128)(2,1)S(1)} %copy-done.9, bf16[768,128]{1,0:T(8,128)(2,1)S(1)} %copy-done.8, f32[128,128]{1,0:T(8,128)S(1)} %copy-done.5, f32[128,128]{1,0:T(8,128)S(1)} %copy-done.4, f32[2,128]{1,0:T(2,128)S(1)} %dynamic-slice_bitcast_fusion.phase), custom_call_target="tpu_custom_call" | custom-call | tf_op jit(solution)/shard_map/channel_forward/pallas_call | solution.py:286
  44.4 0.0 copy-start
  44.4 0.0 copy-start.1
  44.5 0.0 copy-start.2
  44.5 0.0 copy-start.3
  44.5 0.0 copy-start.10
  44.5 0.0 copy-start.11
  44.5 0.0 copy-start.12
  44.5 0.0 copy-start.13
  44.5 36.7 %all_to_all.20 = f32[256,8,128]{2,1,0:T(8,128)S(1)} all-to-all(f32[256,8,128]{2,1,0:T(8,128)S(1)} %bitcast.26), channel_id=1, replica_groups=mesh['tm'=16,'chan'=16] {'tm','chan'}, dimensions={0} | all-to-all | bytes 2097152 | tf_op jit(solution)/shard_map/all_to_all | solution.py:364
  81.2 0.0 copy-done
  81.2 0.0 copy-done.1
  81.2 0.0 copy-done.2
  81.3 4.8 %time_part.1 = f32[2048,128]{1,0:T(8,128)S(1)} custom-call(f32[2048,128]{1,0:T(8,128)S(1)} %bitcast.27, f32[128,1024]{1,0:T(8,128)S(1)} %fusion.1.factor, f32[384,128]{1,0:T(8,128)S(1)} %pad_maximum_fusion.fir, bf16[256,768]{1,0:T(8,128)(2,1)S(1)} %copy-done.3, bf16[256,768]{1,0:T(8,128)(2,1)S(1)} %copy-done.2, f32[128,1024]{1,0:T(8,128)S(1)} %copy-done.1, ...), custom_call_target="tpu_custom_call" | custom-call | tf_op jit(solution)/shard_map/time_part/pallas_call | solution.py:286
  86.1 0.0 copy-start.6
  86.1 0.0 copy-start.7
  86.1 37.1 %all_to_all.21 = f32[256,8,128]{2,1,0:T(8,128)S(1)} all-to-all(f32[256,8,128]{2,1,0:T(8,128)S(1)} %bitcast.28), channel_id=1, replica_groups=mesh['tm'=16,'chan'=16] {'tm','chan'}, dimensions={0} | all-to-all | bytes 2097152 | tf_op jit(solution)/shard_map/all_to_all | solution.py:366
  123.2 0.0 copy-done.6
  123.2 3.3 %channel_inverse.1 = f32[2048,128]{1,0:T(8,128)S(1)} custom-call(f32[2048,128]{1,0:T(8,128)S(1)} %bitcast.24, bf16[128,768]{1,0:T(8,128)(2,1)S(1)} %copy-done.7, bf16[384,256]{1,0:T(8,128)(2,1)S(1)} %copy-done.6, f32[128,128]{1,0:T(8,128)S(1)} %copy-done.5, f32[128,128]{1,0:T(8,128)S(1)} %copy-done.4, f32[2,128]{1,0:T(2,128)S(1)} %dynamic-slice_bitcast_fusion.phase), custom_call_target="tpu_custom_call" | custom-call | tf_op jit(solution)/shard_map/channel_inverse/pallas_call | solution.py:286
  126.5 35.5 %all_to_all.22 = f32[32,64,128]{2,1,0:T(8,128)S(1)} all-to-all(f32[32,64,128]{2,1,0:T(8,128)S(1)} %bitcast.25), channel_id=1, replica_groups={{0,1,2,3,4,5,6,7,8,9,10,11,12,13,14,15,128,129,130,131,132,133,134,135,..., dimensions={0} | all-to-all | bytes 2097152 | tf_op jit(solution)/shard_map/all_to_all | solution.py:368
  161.9 1.1 bitcast_multiply_fusion
  (15 shorter events, 0.2 us)
Async XLA Ops:
  0.0 41.9 %all-to-all-start = ((f32[32,64,128]{2,1,0:T(8,128)}), f32[32,64,128]{2,1,0:T(8,128)S(1)}, u32[]{:S(2)}, u32[]{:S(2)}) async-start(f32[32,64,128]{2,1,0:T(8,128)} %bitcast.29), calls=%async_computation | async-start | bytes 2097152 | tf_op jit(solution)/shard_map/all_to_all | solution.py:361
  11.0 0.8 copy-start.15
  11.9 0.7 copy-start.17
  13.9 0.7 copy-start.16
  13.9 0.7 copy-start.18
  13.9 0.9 copy-start.14
  15.8 26.1 %copy-start.4 = (f32[128,128]{1,0:T(8,128)S(1)}, f32[128,128]{1,0:T(8,128)}, u32[]{:S(2)}) copy-start(f32[128,128]{1,0:T(8,128)} %constant.105.clone.sin) | copy-start | bytes 196612
  15.8 26.1 %copy-start.5 = (f32[128,128]{1,0:T(8,128)S(1)}, f32[128,128]{1,0:T(8,128)}, u32[]{:S(2)}) copy-start(f32[128,128]{1,0:T(8,128)} %constant.104.clone.cos) | copy-start | bytes 196612
  15.8 26.1 %copy-start.8 = (bf16[768,128]{1,0:T(8,128)(2,1)S(1)}, bf16[768,128]{1,0:T(8,128)(2,1)}, u32[]{:S(2)}) copy-start(bf16[768,128]{1,0:T(8,128)(2,1)} %constant.103.clone.second) | copy-start | bytes 589828
  15.8 26.1 %copy-start.9 = (bf16[256,384]{1,0:T(8,128)(2,1)S(1)}, bf16[256,384]{1,0:T(8,128)(2,1)}, u32[]{:S(2)}) copy-start(bf16[256,384]{1,0:T(8,128)(2,1)} %constant.102.clone.first) | copy-start | bytes 589828
  44.4 36.8 %copy-start = (f32[128,1024]{1,0:T(8,128)S(1)}, f32[128,1024]{1,0:T(8,128)}, u32[]{:S(2)}) copy-start(f32[128,1024]{1,0:T(8,128)} %constant.109.clone.sin2) | copy-start | bytes 1572868
  44.4 36.8 %copy-start.1 = (f32[128,1024]{1,0:T(8,128)S(1)}, f32[128,1024]{1,0:T(8,128)}, u32[]{:S(2)}) copy-start(f32[128,1024]{1,0:T(8,128)} %constant.108.clone.cos2) | copy-start | bytes 1572868
  44.5 36.8 %copy-start.2 = (bf16[256,768]{1,0:T(8,128)(2,1)S(1)}, bf16[256,768]{1,0:T(8,128)(2,1)}, u32[]{:S(2)}) copy-start(bf16[256,768]{1,0:T(8,128)(2,1)} %constant.107.clone.inv) | copy-start | bytes 1179652
  44.5 36.8 %copy-start.3 = (bf16[256,768]{1,0:T(8,128)(2,1)S(1)}, bf16[256,768]{1,0:T(8,128)(2,1)}, u32[]{:S(2)}) copy-start(bf16[256,768]{1,0:T(8,128)(2,1)} %constant.106.clone.fwd) | copy-start | bytes 1179652
  44.5 36.8 %copy-start.10 = (f32[1,1024]{1,0:T(1,128)S(1)}, f32[1,1024]{1,0:T(1,128)}, u32[]{:S(2)}) copy-start(f32[1,1024]{1,0:T(1,128)} %constant.113.clone.sin3) | copy-start | bytes 12292
  44.5 36.7 %copy-start.11 = (f32[1,1024]{1,0:T(1,128)S(1)}, f32[1,1024]{1,0:T(1,128)}, u32[]{:S(2)}) copy-start(f32[1,1024]{1,0:T(1,128)} %constant.112.clone.cos3) | copy-start | bytes 12292
  44.5 36.7 %copy-start.12 = (f32[8,128]{1,0:T(8,128)S(1)}, f32[8,128]{1,0:T(8,128)}, u32[]{:S(2)}) copy-start(f32[8,128]{1,0:T(8,128)} %constant.111.clone.sin1) | copy-start | bytes 12292
  44.5 36.7 %copy-start.13 = (f32[8,128]{1,0:T(8,128)S(1)}, f32[8,128]{1,0:T(8,128)}, u32[]{:S(2)}) copy-start(f32[8,128]{1,0:T(8,128)} %constant.110.clone.cos1) | copy-start | bytes 12292
  86.1 37.1 %copy-start.6 = (bf16[384,256]{1,0:T(8,128)(2,1)S(1)}, bf16[384,256]{1,0:T(8,128)(2,1)}, u32[]{:S(2)}) copy-start(bf16[384,256]{1,0:T(8,128)(2,1)} %constant.115.clone.second) | copy-start | bytes 589828
  86.1 37.1 %copy-start.7 = (bf16[128,768]{1,0:T(8,128)(2,1)S(1)}, bf16[128,768]{1,0:T(8,128)(2,1)}, u32[]{:S(2)}) copy-start(bf16[128,768]{1,0:T(8,128)(2,1)} %constant.114.clone.first) | copy-start | bytes 589828

commit v3 on v2

--- a/solution.py
+++ b/solution.py
@@ -27,14 +27,15 @@
 def channel_tables():
     n = np.arange(128)
     cos, sin = circle(n[:, None] * n[None, :], 128)
-    turn_cos, turn_sin = circle(n[:, None] * n[None, :], 16384)
-    first = np.concatenate([cos, -sin], axis=0)
-    second = np.zeros((2, 128, 2, 2, 32))
-    for h in range(2):
+    first = np.concatenate([cos[:64], -sin[:64]], axis=0)
+    first[64] = cos[64]
+    second = np.zeros((2, 128, 4, 2, 32))
+    for h in range(4):
         c, s = cos[:, 32 * h : 32 * h + 32], sin[:, 32 * h : 32 * h + 32]
         second[0, :, h, 0], second[1, :, h, 0] = c, s
         second[0, :, h, 1], second[1, :, h, 1] = -s, c
-    second = second.reshape(256, 128)
+    second = second.reshape(256, 256)
+    turn_cos, turn_sin = circle(np.arange(72)[:, None] * n[None, :], 16384)
     return first, second, turn_cos.astype(np.float32), turn_sin.astype(np.float32)
 
 
@@ -156,36 +157,68 @@
     sin_b[...] = sin[...] * pc + cos[...] * ps
 
 
-def channel_forward(x, first, second, cos, sin, phase, out, cos_b, sin_b):
+def channel_forward(x, first, second, cos, sin, phase, out, cos_b, sin_b, middle):
     turned_tables(cos, sin, phase, cos_b, sin_b)
-    mask = lane_bit(128, 64)
+    mask = lane_bit(64, 64)
+    top = lax.broadcasted_iota(jnp.int32, (64, 128), 0) == 0
+    tables = ((cos, sin), (cos_b, sin_b))
     for rl in range(8):
         early = x[pl.ds(rl, 128, stride=8), :]
         late = x[pl.ds(1024 + rl, 128, stride=8), :]
         y = left_apart(first[...], jnp.concatenate([early + late, early - late], axis=1))
         turned = []
-        for f0, (c, s) in enumerate(((cos[...], sin[...]), (cos_b[...], sin_b[...]))):
-            yr = y[:128, 128 * f0 : 128 * f0 + 128]
-            yi = y[128:, 128 * f0 : 128 * f0 + 128]
+        for f0, (c, s) in enumerate(tables):
+            yr = y[:64, 128 * f0 : 128 * f0 + 128]
+            yi = y[64:, 128 * f0 : 128 * f0 + 128]
+            middle[8 * f0 + rl : 8 * f0 + rl + 1, :] = yi[:1]
+            yi = jnp.where(top, 0.0, yi)
+            c, s = c[:64, :], s[:64, :]
             turned.append(jnp.concatenate([yr * c + yi * s, yi * c - yr * s], axis=1))
         o = right(jnp.concatenate(turned, axis=0), second[...])
-        low, high = exchange(o[:128], o[128:], mask, 64)
-        out[pl.ds(rl, 128, stride=16), :] = low
-        out[pl.ds(8 + rl, 128, stride=16), :] = high
-
-
-def channel_inverse(x, first, second, cos, sin, phase, out, cos_b, sin_b):
+        for half in range(2):
+            cols = slice(128 * half, 128 * half + 128)
+            low, high = exchange(o[:64, cols], o[64:, cols], mask, 64)
+            out[pl.ds(16 * half + rl, 64, stride=32), :] = low
+            out[pl.ds(16 * half + 8 + rl, 64, stride=32), :] = high
+    turned = []
+    for f0, (c, s) in enumerate(tables):
+        y = middle[8 * f0 : 8 * f0 + 8, :]
+        turned.append(jnp.concatenate([y * c[64:65, :], -(y * s[64:65, :])], axis=1))
+    o = right(jnp.concatenate(turned, axis=0), second[...])
+    low, high = exchange(o[:8, :128], o[8:, :128], lane_bit(8, 64), 64)
+    out[16:24, :] = low
+    out[24:32, :] = high
+
+
+def channel_inverse(x, first, second, cos, sin, phase, out, cos_b, sin_b, middle):
     turned_tables(cos, sin, phase, cos_b, sin_b)
-    mask = lane_bit(128, 64)
+    mask = lane_bit(64, 64)
+    top = lax.broadcasted_iota(jnp.int32, (64, 128), 0) == 0
+    tables = ((cos, sin), (cos_b, sin_b))
+    pair = jnp.concatenate(exchange(x[16:24, :], x[24:32, :], lane_bit(8, 64), 64), axis=0)
+    u = right_pair(jnp.concatenate([pair, jnp.zeros_like(pair)], axis=1), second[...])
+    for f0, (c, s) in enumerate(tables):
+        rows = slice(8 * f0, 8 * f0 + 8)
+        middle[rows, :] = u[rows, :128] * c[64:65, :] - u[rows, 128:] * s[64:65, :]
     for rl in range(8):
-        low = x[pl.ds(rl, 128, stride=16), :]
-        high = x[pl.ds(8 + rl, 128, stride=16), :]
-        u = right_pair(jnp.concatenate(exchange(low, high, mask, 64), axis=0), second[...])
+        halves_of = []
+        for half in range(2):
+            low = x[pl.ds(16 * half + rl, 64, stride=32), :]
+            high = x[pl.ds(16 * half + 8 + rl, 64, stride=32), :]
+            pair = jnp.concatenate(exchange(low, high, mask, 64), axis=0)
+            halves_of.append(pair)
+        upper = jnp.concatenate(
+            [jnp.where(top, 0.0, halves_of[1][:64]), jnp.where(top, 0.0, halves_of[1][64:])], axis=0
+        )
+        u = right_pair(jnp.concatenate([halves_of[0], upper], axis=1), second[...])
         turned = []
-        for f0, (c, s) in enumerate(((cos[...], sin[...]), (cos_b[...], sin_b[...]))):
-            ur = u[128 * f0 : 128 * f0 + 128, :128]
-            ui = u[128 * f0 : 128 * f0 + 128, 128:]
-            turned.append(jnp.concatenate([ur * c - ui * s, ui * c + ur * s], axis=0))
+        for f0, (c, s) in enumerate(tables):
+            ur = u[64 * f0 : 64 * f0 + 64, :128]
+            ui = u[64 * f0 : 64 * f0 + 64, 128:]
+            c, s = c[:64, :], s[:64, :]
+            row = middle[8 * f0 + rl : 8 * f0 + rl + 1, :]
+            im = jnp.where(top, row, ui * c + ur * s)
+            turned.append(jnp.concatenate([ur * c - ui * s, im], axis=0))
         o = left_pair(first[...], jnp.concatenate(turned, axis=1))
         out[pl.ds(rl, 128, stride=8), :] = o[:, :128] + o[:, 128:]
         out[pl.ds(1024 + rl, 128, stride=8), :] = o[:, :128] - o[:, 128:]
@@ -296,7 +329,7 @@
 
 def forward_kernel(x, phase):
     first, second, cos, sin = channel_tables()
-    scratch = [pltpu.VMEM((128, 128), f32)] * 2
+    scratch = [pltpu.VMEM((72, 128), f32)] * 2 + [pltpu.VMEM((16, 128), f32)]
     return call(
         channel_forward, (x, left_table(first), right_table(second), cos, sin, phase), scratch
     )
@@ -304,7 +337,7 @@
 
 def inverse_kernel(x, phase):
     first, second, cos, sin = channel_tables()
-    scratch = [pltpu.VMEM((128, 128), f32)] * 2
+    scratch = [pltpu.VMEM((72, 128), f32)] * 2 + [pltpu.VMEM((16, 128), f32)]
     return call(
         channel_inverse, (x, left_table(first.T), right_table(second.T), cos, sin, phase), scratch
     )
@@ -329,10 +362,17 @@
 
 def mask_factor(band_edges, owner, scale):
     spread = (np.arange(32)[:, None] == column_f1()[None, :]).astype(np.float32)
-    edges = band_edges.astype(f32).reshape(256, 32)
+    k1, h = owner // 4, owner % 4
+    conjugate = (h >= 2) & (k1 > 0)
+    mirrored = jnp.roll(band_edges[:, ::-1], 1, axis=1)
+    edges = jnp.where(conjugate, mirrored, band_edges).astype(f32).reshape(256, 32)
     edges = jnp.dot(edges, spread, precision=lax.Precision.HIGHEST)
-    kl = jnp.arange(1024, dtype=jnp.int32) % 32
-    wave = owner // 2 + 128 * (32 * (owner % 2) + kl)
+    k2 = 32 * h + jnp.arange(1024, dtype=jnp.int32) % 32
+    wave = jnp.where(
+        k1 > 0,
+        jnp.where(conjugate, 16384 - k1 - 128 * k2, k1 + 128 * k2),
+        jnp.where(h >= 2, 64 + 128 * (k2 - 64), 128 * k2),
+    )
     wave_f = wave.astype(f32)[None, :]
     kept = (wave_f >= edges[:128]) & (wave_f <= edges[128:])
     weight = jnp.where(wave == 0, scale, 2.0 * scale).astype(f32)[None, :]

time: 163 us -> 162 us (level)
  waiting for transfers between devices: 25.9 us -> 22.1 us
  local copies, waits for them, and re-layouts: 3.52 us -> 7.18 us
    all_to_all x1, waiting for transfers between devices: 25.9 us -> 22.1 us  [per_device(): lax.all_to_all(x, both, 0, 0, tiled=True, axis_index_groups=groups)]
    unnamed x38 -> x42, local copies, waits for them, and re-layouts: 2.28 us -> 5.81 us
  transfers between devices with their start and end apart: 1 -> 1, of which waited for: 1 -> 1; matrix products, arithmetic and copies ran while one was open for 2% -> 3% of each run, Pallas kernels for 0% -> 0%
where the time goes in v3:
time: 162 us
  blocking collectives  109 us (67%)
  waiting for transfers between devices  22.1 us (14%)
  starting transfers between devices  11 us (7%)
  Pallas kernels  9.07 us (6%)
  local copies, waits for them, and re-layouts  7.18 us (4%)
    all_to_all x2, blocking collectives, per_device(): x = lax.all_to_all(x, both, 0, 0, tiled=True).reshape(2048, 128)  73.8 us
    all_to_all x1, blocking collectives, per_device(): x = lax.all_to_all(x, both, 0, 0, tiled=True, axis_index_groups=groups)  35.5 us
    all_to_all x1, waiting for transfers between devices, per_device(): lax.all_to_all(x, both, 0, 0, tiled=True, axis_index_groups=groups)  22.1 us
    all_to_all x1, starting transfers between devices, per_device(): lax.all_to_all(x, both, 0, 0, tiled=True, axis_index_groups=groups)  11 us
    pallas_call x3, Pallas kernels, call(): pl.pallas_call(body, out_shape=jax.ShapeDtypeStruct((2048, 128), f32), in...  9.07 us
    unnamed x42, local copies, waits for them, and re-layouts  5.81 us
  transfers between devices with their start and end apart: 1, of which 1 were waited for; matrix products, arithmetic and copies ran while one was open for 3% of the time, Pallas kernels for 0%

profile of v3, /device:TPU:33, one launch (start us, length us, event | category | flops | bytes accessed | tf_op | source)
XLA Modules:
  0.0 161.5 jit_solution(3095573189315550640)
XLA Ops:
  0.0 11.0 %all-to-all-start = ((f32[32,64,128]{2,1,0:T(8,128)}), f32[32,64,128]{2,1,0:T(8,128)S(1)}, u32[]{:S(2)}, u32[]{:S(2)}) async-start(f32[32,64,128]{2,1,0:T(8,128)} %bitcast.28), calls=%async_computation | async-start | bytes 2097152 | tf_op jit(solution)/shard_map/all_to_all | solution.py:401
  11.0 0.0 copy-start.14
  11.1 0.7 copy-done.14
  11.8 0.1 slice.31
  11.9 2.8 %reverse.2 = s32[2,4096]{1,0:T(2,128)S(1)} reverse(s32[2,4096]{1,0:T(2,128)S(1)} %bitcast.29), dimensions={1} | reverse | bytes 65536
  14.7 0.1 slice.53
  14.8 0.0 slice-start
  14.8 0.6 copy-done.15
  15.5 0.0 slice-done
  15.5 0.1 fusion.2
  15.6 0.1 reshape.67
  15.7 0.0 copy-start.18
  15.8 0.7 copy-done.18
  16.4 0.1 pad_maximum_fusion.1
  16.5 0.3 tile.10
  17.0 0.7 dynamic-slice_bitcast_fusion.phase
  17.7 0.0 copy-start.17
  17.7 0.0 copy-start.19
  17.7 0.0 copy-start.16
  17.8 0.6 copy-done.17
  18.4 0.1 select_reduce_fusion
  18.5 0.1 copy-done.16
  18.6 1.0 fusion.9
  19.6 0.0 copy-start.5
  19.6 0.0 copy-start.6
  19.6 0.0 copy-start.7
  19.6 0.0 copy-start.9
  19.7 0.1 fusion.1.factor
  19.7 22.1 %all-to-all-done = f32[32,64,128]{2,1,0:T(8,128)S(1)} async-done(((f32[32,64,128]{2,1,0:T(8,128)}), f32[32,64,128]{2,1,0:T(8,128)S(1)}, u32[]{:S(2)}, u32[]{:S(2)}) %all-to-all-start) | async-done | bytes 1048608 | tf_op jit(solution)/shard_map/all_to_all | solution.py:401
  41.9 0.0 copy-done.9
  41.9 2.0 %channel_forward.1 = f32[2048,128]{1,0:T(8,128)S(1)} custom-call(f32[2048,128]{1,0:T(8,128)S(1)} %bitcast.22, bf16[128,384]{1,0:T(8,128)(2,1)S(1)} %copy-done.9, bf16[768,256]{1,0:T(8,128)(2,1)S(1)} %copy-done.5, f32[72,128]{1,0:T(8,128)S(1)} %copy-done.7, f32[72,128]{1,0:T(8,128)S(1)} %copy-done.6, f32[2,128]{1,0:T(2,128)S(1)} %dynamic-slice_bitcast_fusion.phase), custom_call_target="tpu_custom_call" | custom-call | tf_op jit(solution)/shard_map/channel_forward/pallas_call | solution.py:319
  43.9 0.0 copy-start
  43.9 0.0 copy-start.1
  43.9 0.0 copy-start.3
  43.9 0.0 copy-start.4
  43.9 0.0 copy-start.10
  43.9 0.0 copy-start.11
  43.9 0.0 copy-start.12
  44.0 0.0 copy-start.13
  44.0 36.7 %all_to_all.20 = f32[256,8,128]{2,1,0:T(8,128)S(1)} all-to-all(f32[256,8,128]{2,1,0:T(8,128)S(1)} %bitcast.25), channel_id=1, replica_groups=mesh['tm'=16,'chan'=16] {'tm','chan'}, dimensions={0} | all-to-all | bytes 2097152 | tf_op jit(solution)/shard_map/all_to_all | solution.py:404
  80.6 0.0 copy-done.1
  80.7 4.8 %time_part.1 = f32[2048,128]{1,0:T(8,128)S(1)} custom-call(f32[2048,128]{1,0:T(8,128)S(1)} %bitcast.26, f32[128,1024]{1,0:T(8,128)S(1)} %fusion.1.factor, f32[384,128]{1,0:T(8,128)S(1)} %pad_maximum_fusion.fir, bf16[256,768]{1,0:T(8,128)(2,1)S(1)} %copy-done.4, bf16[256,768]{1,0:T(8,128)(2,1)S(1)} %copy-done.3, f32[128,1024]{1,0:T(8,128)S(1)} %copy-done.1, ...), custom_call_target="tpu_custom_call" | custom-call | tf_op jit(solution)/shard_map/time_part/pallas_call | solution.py:319
  85.5 0.0 copy-start.2
  85.5 0.0 copy-start.8
  85.5 37.1 %all_to_all.21 = f32[256,8,128]{2,1,0:T(8,128)S(1)} all-to-all(f32[256,8,128]{2,1,0:T(8,128)S(1)} %bitcast.27), channel_id=1, replica_groups=mesh['tm'=16,'chan'=16] {'tm','chan'}, dimensions={0} | all-to-all | bytes 2097152 | tf_op jit(solution)/shard_map/all_to_all | solution.py:406
  122.6 2.3 %channel_inverse.1 = f32[2048,128]{1,0:T(8,128)S(1)} custom-call(f32[2048,128]{1,0:T(8,128)S(1)} %bitcast.23, bf16[128,384]{1,0:T(8,128)(2,1)S(1)} %copy-done.8, bf16[768,256]{1,0:T(8,128)(2,1)S(1)} %copy-done.2, f32[72,128]{1,0:T(8,128)S(1)} %copy-done.7, f32[72,128]{1,0:T(8,128)S(1)} %copy-done.6, f32[2,128]{1,0:T(2,128)S(1)} %dynamic-slice_bitcast_fusion.phase), custom_call_target="tpu_custom_call" | custom-call | tf_op jit(solution)/shard_map/channel_inverse/pallas_call | solution.py:319
  125.0 35.5 %all_to_all.22 = f32[32,64,128]{2,1,0:T(8,128)S(1)} all-to-all(f32[32,64,128]{2,1,0:T(8,128)S(1)} %bitcast.24), channel_id=1, replica_groups={{0,1,2,3,4,5,6,7,8,9,10,11,12,13,14,15,128,129,130,131,132,133,134,135,..., dimensions={0} | all-to-all | bytes 2097152 | tf_op jit(solution)/shard_map/all_to_all | solution.py:408
  160.4 1.1 bitcast_multiply_fusion
  (22 shorter events, 0.2 us)
Async XLA Ops:
  0.0 41.9 %all-to-all-start = ((f32[32,64,128]{2,1,0:T(8,128)}), f32[32,64,128]{2,1,0:T(8,128)S(1)}, u32[]{:S(2)}, u32[]{:S(2)}) async-start(f32[32,64,128]{2,1,0:T(8,128)} %bitcast.28), calls=%async_computation | async-start | bytes 2097152 | tf_op jit(solution)/shard_map/all_to_all | solution.py:401
  11.0 0.8 copy-start.14
  14.7 0.8 copy-start.15
  14.8 0.7 slice-start
  15.7 0.7 copy-start.18
  17.7 0.7 copy-start.17
  17.7 0.7 copy-start.19
  17.7 0.9 copy-start.16
  19.6 22.3 %copy-start.5 = (bf16[768,256]{1,0:T(8,128)(2,1)S(1)}, bf16[768,256]{1,0:T(8,128)(2,1)}, u32[]{:S(2)}) copy-start(bf16[768,256]{1,0:T(8,128)(2,1)} %constant.112.clone.second) | copy-start | bytes 1179652
  19.6 22.3 %copy-start.6 = (f32[72,128]{1,0:T(8,128)S(1)}, f32[72,128]{1,0:T(8,128)}, u32[]{:S(2)}) copy-start(f32[72,128]{1,0:T(8,128)} %constant.114.clone.sin) | copy-start | bytes 110596
  19.6 22.3 %copy-start.7 = (f32[72,128]{1,0:T(8,128)S(1)}, f32[72,128]{1,0:T(8,128)}, u32[]{:S(2)}) copy-start(f32[72,128]{1,0:T(8,128)} %constant.113.clone.cos) | copy-start | bytes 110596
  19.6 22.3 %copy-start.9 = (bf16[128,384]{1,0:T(8,128)(2,1)S(1)}, bf16[128,384]{1,0:T(8,128)(2,1)}, u32[]{:S(2)}) copy-start(bf16[128,384]{1,0:T(8,128)(2,1)} %constant.111.clone.first) | copy-start | bytes 294916
  43.9 36.8 %copy-start = (f32[128,1024]{1,0:T(8,128)S(1)}, f32[128,1024]{1,0:T(8,128)}, u32[]{:S(2)}) copy-start(f32[128,1024]{1,0:T(8,128)} %constant.118.clone.sin2) | copy-start | bytes 1572868
  43.9 36.8 %copy-start.1 = (f32[128,1024]{1,0:T(8,128)S(1)}, f32[128,1024]{1,0:T(8,128)}, u32[]{:S(2)}) copy-start(f32[128,1024]{1,0:T(8,128)} %constant.117.clone.cos2) | copy-start | bytes 1572868
  43.9 36.8 %copy-start.3 = (bf16[256,768]{1,0:T(8,128)(2,1)S(1)}, bf16[256,768]{1,0:T(8,128)(2,1)}, u32[]{:S(2)}) copy-start(bf16[256,768]{1,0:T(8,128)(2,1)} %constant.116.clone.inv) | copy-start | bytes 1179652
  43.9 36.8 %copy-start.4 = (bf16[256,768]{1,0:T(8,128)(2,1)S(1)}, bf16[256,768]{1,0:T(8,128)(2,1)}, u32[]{:S(2)}) copy-start(bf16[256,768]{1,0:T(8,128)(2,1)} %constant.115.clone.fwd) | copy-start | bytes 1179652
  43.9 36.8 %copy-start.10 = (f32[1,1024]{1,0:T(1,128)S(1)}, f32[1,1024]{1,0:T(1,128)}, u32[]{:S(2)}) copy-start(f32[1,1024]{1,0:T(1,128)} %constant.122.clone.sin3) | copy-start | bytes 12292
  43.9 36.7 %copy-start.11 = (f32[1,1024]{1,0:T(1,128)S(1)}, f32[1,1024]{1,0:T(1,128)}, u32[]{:S(2)}) copy-start(f32[1,1024]{1,0:T(1,128)} %constant.121.clone.cos3) | copy-start | bytes 12292
  43.9 36.7 %copy-start.12 = (f32[8,128]{1,0:T(8,128)S(1)}, f32[8,128]{1,0:T(8,128)}, u32[]{:S(2)}) copy-start(f32[8,128]{1,0:T(8,128)} %constant.120.clone.sin1) | copy-start | bytes 12292
  44.0 36.7 %copy-start.13 = (f32[8,128]{1,0:T(8,128)S(1)}, f32[8,128]{1,0:T(8,128)}, u32[]{:S(2)}) copy-start(f32[8,128]{1,0:T(8,128)} %constant.119.clone.cos1) | copy-start | bytes 12292
  85.5 37.1 %copy-start.2 = (bf16[768,256]{1,0:T(8,128)(2,1)S(1)}, bf16[768,256]{1,0:T(8,128)(2,1)}, u32[]{:S(2)}) copy-start(bf16[768,256]{1,0:T(8,128)(2,1)} %constant.124.clone.second) | copy-start | bytes 1179652
  85.5 37.1 %copy-start.8 = (bf16[128,384]{1,0:T(8,128)(2,1)S(1)}, bf16[128,384]{1,0:T(8,128)(2,1)}, u32[]{:S(2)}) copy-start(bf16[128,384]{1,0:T(8,128)(2,1)} %constant.123.clone.first) | copy-start | bytes 294916
